TPU v7x, 256 devices: a whole 4x4x8 slice. The times are simulated.
256 devices in a mesh: role: 2 (over core), exp: 8 (over z), tp: 16 (over x, y).
Axes of the slice: x: 4, y: 4, z: 8, core: 2. Of those that a mesh axis runs over, the one named last changes fastest.
Arguments:
- residual_in: bfloat16 [2048, 8192], P(('role', 'exp', 'tp')), may hold values from -64 to 64
- context: bfloat16 [2048, 8192], P(('role', 'exp'), 'tp'), may hold values from -6 to 6
- out_weight: bfloat16 [8192, 8192], P('tp', ('role', 'exp')), may hold values from -0.0625 to 0.0625
- norm_gain: bfloat16 [8192], replicated, may hold values from 0.5 to 1.5
- router: bfloat16 [2, 4, 8192], replicated, may hold values from -0.125 to 0.125
- up_weight: bfloat16 [2, 8, 8192, 6144], P('role', 'exp', None, 'tp'), may hold values from -0.0625 to 0.0625
- down_weight: bfloat16 [2, 8, 6144, 8192], P('role', 'exp', 'tp'), may hold values from -0.109375 to 0.109375
- modality: int32 [2048], P(('role', 'exp', 'tp')), may hold values from 0 to 1
- expert: int32 [2048], P(('role', 'exp', 'tp')), may hold values from 0 to 3, as said below
Outputs:
- mixed: bfloat16 [2048, 8192], P(('role', 'exp', 'tp'))
Inputs may be any that keep to these rules, and one draw needn't show every extreme that they name: Among the 8 tokens of one device at most 2 choose one expert of one modality, and in every device's tokens some expert of some modality is chosen by exactly 2.
All inputs are finite; a program needn't handle non-finite values.
Results may differ from a plain program's by a relative error of at most 0.0052.
Values may be sent and summed in bfloat16 or wider, within the bound.
A program may use at most 128 MiB of HBM per device.

v0:
```python
import jax
import jax.numpy as jnp
from jax import lax
from jax.sharding import PartitionSpec as P

EXPERTS = 4
CAP = 2


EPSILON = 1e-05


def in_blocks(array, dim, length):
    before, after = (array.shape[:dim], array.shape[dim + 1 :])
    return jnp.moveaxis(array.reshape(*before, length, -1, *after), dim, 0)


def summed_on_arrival(array, axis, dim):
    length = lax.axis_size(axis)
    blocks = lax.all_to_all(in_blocks(array, dim, length), axis, 0, 0, tiled=True)
    return jnp.sum(blocks, axis=0)


def in_order(blocks, dim):
    blocks = jnp.moveaxis(blocks, 0, dim)
    dims = blocks.shape
    return blocks.reshape(*dims[:dim], dims[dim] * dims[dim + 1], *dims[dim + 2 :])


def joined_exchange(array, axis, axes, splits, concats):
    sizes = [lax.axis_size(a) for a in axes]
    blocks = in_blocks(array, splits[0], sizes[0])
    blocks = jnp.moveaxis(in_blocks(blocks, splits[1] + 1, sizes[1]), 0, 1)
    inside = blocks.shape[2:]
    blocks = blocks.reshape(-1, *inside)
    blocks = lax.all_to_all(blocks, axis, split_axis=0, concat_axis=0, tiled=True)
    blocks = in_order(blocks.reshape(*sizes, *inside), concats[0] + 1)
    return in_order(blocks, concats[1])


def per_device(
    residual_in, context, out_weight, norm_gain, router, up_weight, down_weight, modality, expert
):
    tok_rows, width = residual_in.shape
    head_cols = context.shape[1]
    tp_count = lax.axis_size("tp")
    group_count = lax.axis_size("role") * lax.axis_size("exp")
    exp_count = lax.axis_size("exp")
    halves = exp_count // EXPERTS
    grouped = context.reshape(tp_count, tok_rows, head_cols)
    all_rows = lax.all_gather(grouped, ("role", "exp"), axis=1, tiled=True)
    all_rows = all_rows.reshape(tp_count * group_count * tok_rows, head_cols)
    partial_cols = summed_on_arrival(
        jnp.dot(all_rows, out_weight, preferred_element_type=jnp.float32), "tp", 0
    )
    projected = lax.all_to_all(
        partial_cols.reshape(group_count, tok_rows, out_weight.shape[1]),
        ("role", "exp"),
        split_axis=0,
        concat_axis=2,
        tiled=True,
    ).reshape(tok_rows, width)
    resid = (residual_in.astype(jnp.float32) + projected).astype(jnp.bfloat16)
    resid = lax.optimization_barrier(resid)
    widened = resid.astype(jnp.float32)
    inverse_rms = lax.rsqrt(jnp.mean(widened * widened, axis=-1, keepdims=True) + EPSILON)
    normed = (widened * inverse_rms * norm_gain.astype(jnp.float32)).astype(jnp.bfloat16)
    routes = modality * EXPERTS + expert
    choices_hot = routes[:, None] == jnp.arange(2 * EXPERTS, dtype=jnp.int32)[None, :]
    hot_ints = choices_hot.astype(jnp.int32)
    earlier = jnp.cumsum(hot_ints, axis=0) - hot_ints
    position = jnp.sum(earlier * hot_ints, axis=1)
    target = routes * CAP + position
    placed = (jnp.arange(2 * EXPERTS * CAP, dtype=jnp.int32)[:, None] == target[None, :]).astype(
        jnp.bfloat16
    )
    placed = placed.reshape(2, EXPERTS, CAP, tok_rows)
    logits = lax.dot_general(
        normed,
        router.reshape(2 * EXPERTS, width),
        (((1,), (1,)), ((), ())),
        preferred_element_type=jnp.float32,
    )
    gating = jax.nn.sigmoid(jnp.sum(jnp.where(choices_hot, logits, 0.0), axis=1))
    slotted = jnp.einsum("mecq,qd->mecd", placed, normed, preferred_element_type=jnp.float32)
    slotted = slotted.astype(jnp.bfloat16)
    outgoing = jnp.broadcast_to(slotted[:, :, None], (2, EXPERTS, halves, CAP, width))
    outgoing = outgoing.reshape(2, exp_count, CAP, width)
    incoming = joined_exchange(outgoing, ("role", "exp"), ("role", "exp"), (0, 1), (0, 1))
    local_slots = incoming.reshape(2 * exp_count * CAP, width)
    up_matrix = up_weight[0, 0]
    down_matrix = down_weight[0, 0]
    up_sums = jnp.dot(
        lax.all_gather(local_slots, "tp", axis=0, tiled=True),
        up_matrix,
        preferred_element_type=jnp.float32,
    )
    hidden = jax.nn.gelu(up_sums).astype(jnp.bfloat16)
    results = lax.psum_scatter(
        jnp.dot(hidden, down_matrix, preferred_element_type=jnp.float32),
        "tp",
        scatter_dimension=0,
        tiled=True,
    )
    returned = joined_exchange(
        results.reshape(2, exp_count, CAP, width).astype(jnp.bfloat16),
        ("role", "exp"),
        ("role", "exp"),
        (0, 1),
        (0, 1),
    ).astype(jnp.float32)
    expert_out = jnp.einsum(
        "mecq,mescd->qd",
        placed.astype(jnp.float32),
        returned.reshape(2, EXPERTS, halves, CAP, width),
        precision=lax.Precision.HIGHEST,
    )
    return (widened + gating[:, None] * expert_out).astype(jnp.bfloat16)


def solution(mesh):
    in_specs = (
        P(("role", "exp", "tp"), None),
        P(("role", "exp"), "tp"),
        P("tp", ("role", "exp")),
        P(),
        P(),
        P("role", "exp", None, "tp"),
        P("role", "exp", "tp", None),
        P(("role", "exp", "tp")),
        P(("role", "exp", "tp")),
    )
    out_specs = P(("role", "exp", "tp"), None)
    return jax.shard_map(
        per_device, mesh=mesh, in_specs=in_specs, out_specs=out_specs, check_vma=False
    )
```

profile of v0, /device:TPU:1, one launch (start us, length us, event | category | flops | bytes accessed | tf_op | source)
XLA Modules:
  0.0 412.3 jit_solution(11668320973444184488)
XLA Ops:
  6.5 0.0 copy-start
  6.5 0.0 all-gather.3.cloned.1.call-start
  6.5 0.7 all-gather.3.cloned.1.call-update
  7.3 0.0 copy-start.4
  7.3 0.0 copy-start.5
  7.3 45.6 %all-gather.3.cloned.1.call-done = bf16[16,128,512]{2,1,0:T(8,128)(2,1)} async-done(((bf16[16,8,512]{2,1,0:T(8,128)(2,1)}), bf16[16,128,512]{2,1,0:T(8,128)(2,1)}) %all-gather.3.cloned.1.call-update) | async-done | bytes 2097168 | tf_op jit(solution)/shard_map/all_gather | solution.py:51
  52.9 0.0 copy-done
  52.9 4.8 %fusion.20 = f32[16,128,512]{2,1,0:T(8,128)} fusion(bf16[16,128,512]{2,1,0:T(8,128)(2,1)} %all-gather.3.cloned.1.call-done, bf16[512,512]{1,0:T(8,128)(2,1)S(1)} %copy-done), kind=kOutput, calls=%fused_computation.21 | convolution fusion | flops 1073741824 | bytes 6815744 | tf_op jit(solution)/shard_map/dot_general | solution.py:54
  57.7 0.0 copy-start.3
  57.7 0.0 copy-start.2
  57.7 6.7 %all-to-all-start = ((f32[16,128,512]{2,1,0:T(8,128)}), f32[16,128,512]{2,1,0:T(8,128)}, u32[]{:S(2)}, u32[]{:S(2)}) async-start(f32[16,128,512]{2,1,0:T(8,128)} %fusion.20), calls=%async_computation | async-start | bytes 8388608 | tf_op jit(solution)/shard_map/all_to_all | solution.py:20
  64.4 0.0 copy-done.4
  64.4 0.0 copy-done.5
  64.4 55.5 %all-to-all-done = f32[16,128,512]{2,1,0:T(8,128)} async-done(((f32[16,128,512]{2,1,0:T(8,128)}), f32[16,128,512]{2,1,0:T(8,128)}, u32[]{:S(2)}, u32[]{:S(2)}) %all-to-all-start) | async-done | bytes 4194336 | tf_op jit(solution)/shard_map/all_to_all | solution.py:20
  120.0 3.3 reduce_sum.45
  123.3 5.3 %all-to-all-start.1 = ((f32[16,8,512]{2,1,0:T(8,128)}), f32[16,8,512]{2,1,0:T(8,128)S(1)}, u32[]{:S(2)}, u32[]{:S(2)}) async-start(f32[16,8,512]{2,1,0:T(8,128)} %bitcast.2), calls=%async_computation.1 | async-start | bytes 524288 | tf_op jit(solution)/shard_map/all_to_all | solution.py:56
  128.6 0.0 all-gather.5.cloned.1.call-start
  128.6 0.0 copy-done.3
  128.6 0.2 reduce_window_sum.11
  128.8 9.4 %all-to-all-done.1 = f32[16,8,512]{2,1,0:T(8,128)S(1)} async-done(((f32[16,8,512]{2,1,0:T(8,128)}), f32[16,8,512]{2,1,0:T(8,128)S(1)}, u32[]{:S(2)}, u32[]{:S(2)}) %all-to-all-start.1) | async-done | bytes 262176 | tf_op jit(solution)/shard_map/all_to_all | solution.py:56
  138.2 0.0 copy-done.2
  138.2 0.2 fusion.23
  138.4 0.3 convolution_convert_fusion
  138.7 0.3 copy.13
  139.0 0.4 broadcast_in_dim.6
  139.4 19.5 %all_to_all.30 = bf16[16,1,1,2,8192]{4,3,2,1,0:T(2,128)(2,1)S(1)} all-to-all(bf16[16,1,1,2,8192]{4,3,2,1,0:T(2,128)(2,1)S(1)} %bitcast.64), channel_id=1, replica_groups=mesh['role'=2,'exp'=8,'tp'=16] {'role','exp'}, dimensions={0} | all-to-all | bytes 1048576 | tf_op jit(solution)/shard_map/all_to_all | solution.py:36
  158.9 1.0 reshape_reshape.3
  159.9 0.0 all-gather.5.cloned.1.call-update
  160.0 0.0 reduce-scatter.2.cloned.1.call-start
  160.0 82.0 %all-gather.5.cloned.1.call-done = bf16[512,8192]{1,0:T(8,128)(2,1)} async-done(((bf16[32,8192]{1,0:T(8,128)(2,1)}), bf16[512,8192]{1,0:T(8,128)(2,1)}) %all-gather.5.cloned.1.call-update) | async-done | bytes 8388624 | tf_op jit(solution)/shard_map/all_gather | solution.py:94
  242.0 9.8 %fusion.17 = bf16[512,384]{1,0:T(8,128)(2,1)S(1)} fusion(bf16[512,8192]{1,0:T(8,128)(2,1)} %all-gather.5.cloned.1.call-done, bf16[1,1,8192,384]{3,2,1,0:T(8,128)(2,1)} %param.14), kind=kOutput, calls=%fused_computation.20 | convolution fusion | flops 3222994944 | bytes 15073280 | tf_op jit(solution)/shard_map/dot_general | solution.py:93
  251.8 10.9 %fusion.3 = f32[512,8192]{1,0:T(8,128)} fusion(bf16[512,384]{1,0:T(8,128)(2,1)S(1)} %fusion.17, bf16[1,1,384,8192]{3,2,1,0:T(8,128)(2,1)} %param.15), kind=kOutput, calls=%fused_computation.5 | convolution fusion | flops 3221225472 | bytes 23461888 | tf_op jit(solution)/shard_map/dot_general | solution.py:100
  262.7 0.0 copy-start.1
  262.7 0.0 reduce-scatter.2.cloned.1.call-update
  262.8 115.6 %reduce-scatter.2.cloned.1.call-done = f32[32,8192]{1,0:T(8,128)} async-done(((f32[512,8192]{1,0:T(8,128)}), f32[32,8192]{1,0:T(8,128)}) %reduce-scatter.2.cloned.1.call-update) | async-done | bytes 1048592 | tf_op jit(solution)/shard_map/reduce_scatter | solution.py:99
  378.3 1.3 convert_element_type.70
  379.6 1.1 convert_element_type.71
  380.7 8.0 %all-to-all-start.3 = ((bf16[16,1,1,2,8192]{4,3,2,1,0:T(2,128)(2,1)}), bf16[16,1,1,2,8192]{4,3,2,1,0:T(2,128)(2,1)S(1)}, u32[]{:S(2)}, u32[]{:S(2)}) async-start(bf16[16,1,1,2,8192]{4,3,2,1,0:T(2,128)(2,1)} %bitcast.15), calls=%async_computation.4 | async-start | bytes 1048576 | tf_op jit(solution)/shard_map/all_to_all | solution.py:36
  388.8 0.0 copy-done.1
  388.8 0.3 fusion.7
  389.1 14.4 %all-to-all-done.3 = bf16[16,1,1,2,8192]{4,3,2,1,0:T(2,128)(2,1)S(1)} async-done(((bf16[16,1,1,2,8192]{4,3,2,1,0:T(2,128)(2,1)}), bf16[16,1,1,2,8192]{4,3,2,1,0:T(2,128)(2,1)S(1)}, u32[]{:S(2)}, u32[]{:S(2)}) %all-to-all-start.3) | async-done | bytes 524320 | tf_op jit(solution)/shard_map/all_to_all | solution.py:36
  403.5 0.6 convert_reduce_fusion
  404.2 1.6 fusion.2
  (10 shorter events, 0.1 us)
Async XLA Ops:
  6.5 46.3 %copy-start = (bf16[512,512]{1,0:T(8,128)(2,1)S(1)}, bf16[512,512]{1,0:T(8,128)(2,1)}, u32[]{:S(2)}) copy-start(bf16[512,512]{1,0:T(8,128)(2,1)} %param.11) | copy-start | bytes 1572868
  6.5 46.3 %all-gather.3.cloned.1.call-start = ((), (), s32[]{:S(2)}) async-start(), calls=%async_computation.5 | async-start | bytes 2228224 | tf_op jit(solution)/shard_map/all_gather | solution.py:51
  7.3 57.2 %copy-start.4 = (s32[8]{0:T(128)S(1)}, s32[8]{0:T(128)}, u32[]{:S(2)}) copy-start(s32[8]{0:T(128)} %param.17) | copy-start | bytes 100
  7.3 57.2 %copy-start.5 = (s32[8]{0:T(128)S(1)}, s32[8]{0:T(128)}, u32[]{:S(2)}) copy-start(s32[8]{0:T(128)} %param.16) | copy-start | bytes 100
  57.7 70.9 %copy-start.3 = (bf16[8192]{0:T(1024)(128)(2,1)S(1)}, bf16[8192]{0:T(1024)(128)(2,1)}, u32[]{:S(2)}) copy-start(bf16[8192]{0:T(1024)(128)(2,1)} %param.12) | copy-start | bytes 49156
  57.7 80.5 %copy-start.2 = (bf16[8,8192]{1,0:T(8,128)(2,1)S(1)}, bf16[8,8192]{1,0:T(8,128)(2,1)}, u32[]{:S(2)}) copy-start(bf16[8,8192]{1,0:T(8,128)(2,1)} %param.9) | copy-start | bytes 393220
  57.7 62.3 %all-to-all-start = ((f32[16,128,512]{2,1,0:T(8,128)}), f32[16,128,512]{2,1,0:T(8,128)}, u32[]{:S(2)}, u32[]{:S(2)}) async-start(f32[16,128,512]{2,1,0:T(8,128)} %fusion.20), calls=%async_computation | async-start | bytes 8388608 | tf_op jit(solution)/shard_map/all_to_all | solution.py:20
  123.3 14.9 %all-to-all-start.1 = ((f32[16,8,512]{2,1,0:T(8,128)}), f32[16,8,512]{2,1,0:T(8,128)S(1)}, u32[]{:S(2)}, u32[]{:S(2)}) async-start(f32[16,8,512]{2,1,0:T(8,128)} %bitcast.2), calls=%async_computation.1 | async-start | bytes 524288 | tf_op jit(solution)/shard_map/all_to_all | solution.py:56
  128.6 113.5 %all-gather.5.cloned.1.call-start = ((), (), s32[]{:S(2)}) async-start(), calls=%async_computation.6 | async-start | bytes 8912896 | tf_op jit(solution)/shard_map/all_gather | solution.py:94
  160.0 218.4 %reduce-scatter.2.cloned.1.call-start = ((), (), s32[]{:S(2)}) async-start(), calls=%async_computation.7 | async-start | bytes 17825792 | tf_op jit(solution)/shard_map/reduce_scatter | solution.py:99
  262.7 126.0 %copy-start.1 = (bf16[2,4,8192]{2,1,0:T(4,128)(2,1)S(1)}, bf16[2,4,8192]{2,1,0:T(4,128)(2,1)}, u32[]{:S(2)}) copy-start(bf16[2,4,8192]{2,1,0:T(4,128)(2,1)} %param.13) | copy-start | bytes 393220
  380.7 22.8 %all-to-all-start.3 = ((bf16[16,1,1,2,8192]{4,3,2,1,0:T(2,128)(2,1)}), bf16[16,1,1,2,8192]{4,3,2,1,0:T(2,128)(2,1)S(1)}, u32[]{:S(2)}, u32[]{:S(2)}) async-start(bf16[16,1,1,2,8192]{4,3,2,1,0:T(2,128)(2,1)} %bitcast.15), calls=%async_computation.4 | async-start | bytes 1048576 | tf_op jit(solution)/shard_map/all_to_all | solution.py:36
Sparse Core Ops, SparseCore 0:
  9.2 43.6 all-gather.2
  160.1 81.9 all-gather.4
  262.9 115.4 reduce-scatter.1
where the time goes:
time: 413 us; the launch traced here: 412 us
  waiting for transfers between devices  323 us (78%)
  matrix products  27.7 us (7%)
  starting transfers between devices  20.1 us (5%)
  blocking collectives  19.5 us (5%)
  between operations  13.2 us (3%)
  other arithmetic  5.66 us (1%)
    reduce_scatter x1, waiting for transfers between devices, per_device(): lax.psum_scatter(jnp.dot(hidden, down_matrix, preferred_element_type=jnp....  116 us
    all_gather x1, waiting for transfers between devices, per_device(): lax.all_gather(local_slots, 'tp', axis=0, tiled=True)  82 us
    all_to_all x1, waiting for transfers between devices, summed_on_arrival(): lax.all_to_all(in_blocks(array, dim, length), axis, 0, 0, tiled=True)  55.5 us
    all_gather x1, waiting for transfers between devices, per_device(): all_rows = lax.all_gather(grouped, ('role', 'exp'), axis=1, tiled=True)  45.6 us
    all_to_all x1, blocking collectives, joined_exchange(): lax.all_to_all(blocks, axis, split_axis=0, concat_axis=0, tiled=True)  19.5 us
    all_to_all x1, waiting for transfers between devices, joined_exchange(): lax.all_to_all(blocks, axis, split_axis=0, concat_axis=0, tiled=True)  14.4 us
    dot_general x1, matrix products, per_device(): jnp.dot(hidden, down_matrix, preferred_element_type=jnp.float32)  10.9 us
    dot_general x1, matrix products, per_device(): jnp.dot(lax.all_gather(local_slots, 'tp', axis=0, tiled=True), up_matrix,...  9.77 us
  transfers between devices with their start and end apart: 6, of which 6 were waited for; matrix products, arithmetic and copies ran while one was open for 0% of the time, Pallas kernels for 0%

commit v1 on v0

v1 whole, which is shorter than its diff:
```python
import functools

import jax
import jax.numpy as jnp
from jax import lax
from jax.experimental import pallas as pl
from jax.experimental.pallas import tpu as pltpu
from jax.sharding import PartitionSpec as P

EXPERTS = 4
CAP = 2
EPSILON = 1e-05
SIDE = 4
NSEM = 224
f32, bf16 = jnp.float32, jnp.bfloat16
MESH = pl.DeviceIdType.MESH


class Sums:
    def __init__(self, send, near, src, q, f, s, q2, f2):
        self.send, self.near = send, near
        self.src, self.q, self.f, self.s, self.q2, self.f2 = src, q, f, s, q2, f2
        self.width = src.shape[3]
        self.part = self.width // 4
        self.m, self.n = {}, {}

    def sel(self, h, k, c, w):
        cols = pl.ds(c, w)
        return self.src.at[:, k, :, cols] if h == 0 else self.src.at[k, :, :, cols]

    def base(self, h):
        return h * 2 * self.part

    def s1(self, h, quarter):
        p, a = self.part, self.base(h)
        plus, minus = self.near(1 - h, 1), self.near(1 - h, -1)
        if quarter == 0:
            self.m[h, 1] = self.send(self.sel(h, 2, a, p), self.q.at[h * 2], plus)
            self.m[h, 4] = self.send(self.sel(h, 3, a, p), self.f.at[h, 1, :, :, pl.ds(0, p)], minus)
        else:
            self.m[h, 2] = self.send(self.sel(h, 2, a + p, p), self.q.at[h * 2 + 1], minus)
            self.m[h, 3] = self.send(self.sel(h, 1, a + p, p), self.f.at[h, 0, :, :, pl.ds(p, p)], plus)

    def s2(self, h, quarter):
        p, a = self.part, self.base(h)
        k, c, which = (1, a, 1) if quarter == 0 else (3, a + p, 2)
        got = self.q.at[h * 2 + quarter]
        self.m[h, which].wait_recv()
        cols = pl.ds(c, p)

        def body(i, _):
            at = (i, k, slice(None), cols) if h == 0 else (k, i, slice(None), cols)
            self.src[at] = (self.src[at].astype(f32) + got[i].astype(f32)).astype(bf16)
            return 0

        lax.fori_loop(0, SIDE, body, 0)
        if quarter == 0:
            self.m[h, 5] = self.send(self.sel(h, 1, c, p), self.f.at[h, 0, :, :, pl.ds(0, p)], self.near(1 - h, 1))
        else:
            self.m[h, 6] = self.send(self.sel(h, 3, c, p), self.f.at[h, 1, :, :, pl.ds(p, p)], self.near(1 - h, -1))

    def s3(self, h):
        for i in (3, 4, 5, 6):
            self.m[h, i].wait_recv()
        p = self.part
        cols = pl.ds(self.base(h), 2 * p)

        def body(i, _):
            at = (i, 0, slice(None), cols) if h == 0 else (0, i, slice(None), cols)
            total = self.src[at].astype(f32) + self.f[h, 0, i].astype(f32) + self.f[h, 1, i].astype(f32)
            self.s[h, i] = total.astype(bf16)
            return 0

        lax.fori_loop(0, SIDE, body, 0)
        plus, minus = self.near(h, 1), self.near(h, -1)
        lo, hi = pl.ds(0, p), pl.ds(p, p)
        self.n[h, 1] = self.send(self.s.at[h, 2, :, lo], self.q2.at[h * 2], plus)
        self.n[h, 2] = self.send(self.s.at[h, 2, :, hi], self.q2.at[h * 2 + 1], minus)
        self.n[h, 3] = self.send(self.s.at[h, 1, :, hi], self.f2.at[h, 0, :, hi], plus)
        self.n[h, 4] = self.send(self.s.at[h, 3, :, lo], self.f2.at[h, 1, :, lo], minus)

    def s5(self, h):
        p = self.part
        lo, hi = pl.ds(0, p), pl.ds(p, p)
        self.n[h, 1].wait_recv()
        self.s[h, 1, :, lo] = (self.s[h, 1, :, lo].astype(f32) + self.q2[h * 2].astype(f32)).astype(bf16)
        self.n[h, 5] = self.send(self.s.at[h, 1, :, lo], self.f2.at[h, 0, :, lo], self.near(h, 1))
        self.n[h, 2].wait_recv()
        self.s[h, 3, :, hi] = (self.s[h, 3, :, hi].astype(f32) + self.q2[h * 2 + 1].astype(f32)).astype(bf16)
        self.n[h, 6] = self.send(self.s.at[h, 3, :, hi], self.f2.at[h, 1, :, hi], self.near(h, -1))

    def s6(self, h):
        for i in (3, 4, 5, 6):
            self.n[h, i].wait_recv()
        return self.s[h, 0].astype(f32) + self.f2[h, 0].astype(f32) + self.f2[h, 1].astype(f32)


class Gather:
    def __init__(self, send, near, dst):
        self.send, self.near, self.dst = send, near, dst
        self.part = dst.shape[3] // 4
        self.m = {}

    def blk(self, h, a, b, c, w):
        i, j = (a, b) if h == 0 else (b, a)
        return self.dst.at[i, j, :, pl.ds(h * 2 * self.part + c, w)]

    def first(self, h, name, a, b, c, w, sign, a2):
        self.m[h, name] = self.send(self.blk(h, a, b, c, w), self.blk(h, a2, b, c, w), self.near(h, sign))

    def second(self, h, name, a, b, c, w, sign, b2):
        self.m[h, name] = self.send(self.blk(h, a, b, c, w), self.blk(h, a, b2, c, w), self.near(1 - h, sign))

    def across(self, h, a):
        p = self.part
        self.second(h, ("p", a), a, 0, 0, 2 * p, 1, 3)
        self.second(h, ("m", a), a, 0, 0, 2 * p, -1, 1)

    def begin(self):
        p = self.part
        for h in (0, 1):
            self.first(h, "p", 0, 0, 0, 2 * p, 1, 3)
            self.first(h, "m", 0, 0, 0, 2 * p, -1, 1)
        for h in (0, 1):
            self.across(h, 0)

    def step1(self, h):
        p = self.part
        self.m[h, "p"].wait_recv()
        self.first(h, "pp", 3, 0, 0, p, 1, 2)
        self.m[h, "m"].wait_recv()
        self.first(h, "mm", 1, 0, p, p, -1, 2)
        self.across(h, 3)
        self.across(h, 1)

    def onward(self, h, a):
        p = self.part
        self.m[h, ("p", a)].wait_recv()
        self.second(h, ("pp", a), a, 3, 0, p, 1, 2)
        self.m[h, ("m", a)].wait_recv()
        self.second(h, ("mm", a), a, 1, p, p, -1, 2)

    def step3(self, h):
        self.m[h, "pp"].wait_recv()
        self.m[h, "mm"].wait_recv()
        self.across(h, 2)

    def end(self):
        for h in (0, 1):
            for a in range(SIDE):
                self.m[h, ("pp", a)].wait_recv()
                self.m[h, ("mm", a)].wait_recv()


def kernel(
    depth, residual, context, out_weight, gain, router, mask, pick, put, unfold, fold, up_hbm, down_hbm, out,
    cg, res, p1, p1q, p1f, p1s, p1q2, p1f2, tiles, heads, resid, folded, outgoing, arrived,
    grid, up, down, acc, hidden, part, rq, rf, rs, rq2, rf2, back, returned, ssem, rsem, wsem,
):
    r, z, t = lax.axis_index("role"), lax.axis_index("exp"), lax.axis_index("tp")
    x, y = t // SIDE, t % SIDE
    width = out.shape[1]
    fold_cols = width // 8
    count = [0]
    sent = []

    def send(src, dst, device):
        k = count[0]
        count[0] += 1
        copy = pltpu.make_async_remote_copy(
            src_ref=src, dst_ref=dst, send_sem=ssem.at[k], recv_sem=rsem.at[k], device_id=device, device_id_type=MESH
        )
        copy.start()
        sent.append(copy)
        return copy

    class Local:
        def __init__(self, src, dst):
            k = count[0]
            count[0] += 1
            self.copy = pltpu.make_async_copy(src, dst, rsem.at[k])
            self.copy.start()

        def wait_recv(self):
            self.copy.wait()

    def near(axis, step):
        if axis == 0:
            return (r, z, lax.rem(x + step + SIDE, SIDE) * SIDE + y)
        return (r, z, x * SIDE + lax.rem(y + step + SIDE, SIDE))

    def peer(dr, dz):
        return (lax.rem(r + dr, 2), lax.rem(z + dz + depth, depth), t)

    loads = [pltpu.make_async_copy(up_hbm, up, wsem.at[0]), pltpu.make_async_copy(down_hbm, down, wsem.at[1])]
    for load in loads:
        load.start()

    barrier = pltpu.get_barrier_semaphore()
    others = [peer(dr, dz) for dz in range(depth) for dr in (0, 1) if (dr, dz) != (0, 0)]
    others += [near(axis, step) for axis in (0, 1) for step in (1, -1)]
    for device in others:
        pl.semaphore_signal(barrier, inc=1, device_id=device, device_id_type=MESH)
    pl.semaphore_wait(barrier, len(others))

    rows = context.shape[0]
    mid = depth // 2
    partner = peer(1, 0)
    up_z, down_z = peer(0, 1), peer(0, -1)
    shared = {0: send(context, cg.at[0, 1], partner)}
    going = send(context, cg.at[depth - 1, 0], up_z)
    coming = send(context, cg.at[1, 0], down_z)

    def project(dz, own):
        shared[dz].wait_recv()
        both = jnp.concatenate([own, cg[dz, 1]], axis=0)
        res[...] = jnp.dot(both, out_weight[...], preferred_element_type=f32)

        def body(i, _):
            dx, dy = i // SIDE, i % SIDE
            home = lax.rem(x + dx, SIDE) * SIDE + lax.rem(y + dy, SIDE)
            at = pl.multiple_of(home * 8, 8)
            block = jnp.concatenate([res[pl.ds(at, 8), :], res[pl.ds(rows + at, 8), :]], axis=0)
            p1[dx, dy, pl.ds(dz * 16, 16), :] = block.astype(bf16)
            return 0

        lax.fori_loop(0, SIDE * SIDE, body, 0)

    half_rows = rows // 2
    pending = [0]
    for step in range(1, mid):
        a, b = depth - step, step
        going.wait_recv()
        if step < mid - 1:
            going_next = send(cg.at[a, 0], cg.at[a - 1, 0], up_z)
        else:
            going_next = send(cg.at[a, 0, pl.ds(0, half_rows)], cg.at[mid, 0, pl.ds(0, half_rows)], up_z)
        shared[a] = send(cg.at[a, 0], cg.at[a, 1], partner)
        coming.wait_recv()
        if step < mid - 1:
            coming_next = send(cg.at[b, 0], cg.at[b + 1, 0], down_z)
        else:
            coming_next = send(cg.at[b, 0, pl.ds(half_rows, half_rows)], cg.at[mid, 0, pl.ds(half_rows, half_rows)], down_z)
        shared[b] = send(cg.at[b, 0], cg.at[b, 1], partner)
        going, coming = going_next, coming_next
        for dz in pending:
            project(dz, context[...] if dz == 0 else cg[dz, 0])
        pending = [a, b]
    going.wait_recv()
    coming.wait_recv()
    shared[mid] = send(cg.at[mid, 0], cg.at[mid, 1], partner)
    for dz in pending + [mid]:
        project(dz, cg[dz, 0])

    heads_sum = Sums(send, near, p1, p1q, p1f, p1s, p1q2, p1f2)
    for quarter in (0, 1):
        for h in (0, 1):
            heads_sum.s1(h, quarter)
    for quarter in (0, 1):
        for h in (0, 1):
            heads_sum.s2(h, quarter)
    for h in (0, 1):
        heads_sum.s3(h)
    for h in (0, 1):
        heads_sum.s5(h)
    final = [heads_sum.s6(h) for h in (0, 1)]
    for i in range(2 * depth):
        tiles[i] = jnp.concatenate([final[0][8 * i : 8 * i + 8], final[1][8 * i : 8 * i + 8]], axis=0).astype(bf16)

    mine = r * depth + z
    columns = []
    for dz in range(depth):
        for dr in (0, 1):
            src, dst = tiles.at[dz * 2 + dr], heads.at[mine]
            columns.append(Local(src, dst) if (dr, dz) == (0, 0) else send(src, dst, peer(dr, dz)))
    for copy in columns:
        copy.wait_recv()
    group = width // (2 * depth)
    squares = jnp.zeros((8, group), f32)
    for g in range(2 * depth):
        block = heads[g].astype(f32)
        whole = jnp.concatenate([block[:8], block[8:]], axis=1)
        cols = slice(g * group, (g + 1) * group)
        value = (residual[:, cols].astype(f32) + whole).astype(bf16).astype(f32)
        resid[:, cols] = value
        squares = squares + value * value
    inverse = lax.rsqrt(jnp.sum(squares, axis=1, keepdims=True) / width + EPSILON)
    logits = jnp.zeros((8, fold_cols), f32)
    choice = mask[...]
    for j in range(0, 8, 2):
        pair = []
        for i in (j, j + 1):
            cols = slice(i * fold_cols, (i + 1) * fold_cols)
            normed = (resid[:, cols] * inverse * gain[:, cols].astype(f32)).astype(bf16).astype(f32)
            rows_of = router[:, cols].astype(f32)
            picked = choice[:, 0:1] * rows_of[0:1]
            for e in range(1, 2 * EXPERTS):
                picked = picked + choice[:, e : e + 1] * rows_of[e : e + 1]
            logits = logits + normed * picked
            pair.append(normed)
        folded[pl.ds(j * 8, 16), :] = jnp.concatenate(pair, axis=0).astype(bf16)
    slots = jnp.dot(pick[...], folded[...], preferred_element_type=f32).astype(bf16)
    outgoing[...] = slots.reshape(outgoing.shape)
    gating = jax.nn.sigmoid(jnp.sum(logits, axis=1, keepdims=True))

    halves = depth // EXPERTS
    dispatched = {}
    for dr in (0, 1):
        for dz in range(depth):
            to = peer(dr, dz)
            src, dst = outgoing.at[to[0] * EXPERTS + to[1] // halves], arrived.at[dr, dz]
            dispatched[dr, dz] = Local(src, dst) if (dr, dz) == (0, 0) else send(src, dst, to)

    gathers = [Gather(send, near, grid.at[w]) for w in (0, 1)]
    sums = [
        Sums(send, near, part.at[w], rq.at[w], rf.at[w], rs.at[w], rq2.at[w], rf2.at[w]) for w in (0, 1)
    ]
    slot_rows = 2 * depth

    def enter(w):
        for dz in range(depth):
            dispatched[w, dz].wait_recv()
        block = arrived[w].reshape(8 * slot_rows, fold_cols)
        lines = jnp.dot(unfold[...], block, preferred_element_type=f32).astype(bf16)
        for j in range(8):
            grid[w, 0, 0, :, pl.ds(j * fold_cols, fold_cols)] = lines[j * slot_rows : (j + 1) * slot_rows]
        gathers[w].begin()

    many = SIDE * SIDE * slot_rows
    chunk = width // 16

    def up_piece(w, piece):
        if piece == 0:
            acc[...] = jnp.zeros_like(acc)

        def body(i, _):
            at = pl.ds(pl.multiple_of(i * chunk, chunk), chunk)
            acc[...] += jnp.dot(
                grid[w, :, :, :, at].reshape(many, chunk), up[at, :], preferred_element_type=f32
            )
            return 0

        lax.fori_loop(piece * 4, piece * 4 + 4, body, 0)
        if piece == 3:
            hidden[...] = jax.nn.gelu(acc[...]).astype(bf16)

    def down_piece(w, quarter):
        def body(i, _):
            at = pl.ds(pl.multiple_of(i * chunk, chunk), chunk)
            got = jnp.dot(hidden[...], down[:, at], preferred_element_type=f32)
            part[w, :, :, :, at] = got.astype(bf16).reshape(SIDE, SIDE, slot_rows, chunk)
            return 0

        lax.fori_loop(quarter * 4, quarter * 4 + 4, body, 0)

    def down_and_send(w):
        for quarter in (0, 1):
            for h in (0, 1):
                down_piece(w, 2 * h + quarter)
                sums[w].s1(h, quarter)

    returns = {}

    def leave(w):
        lines = []
        for h in (0, 1):
            total = sums[w].s6(h)
            lines += [total[:, j * fold_cols : (j + 1) * fold_cols] for j in range(4)]
        block = jnp.concatenate(lines, axis=0).astype(bf16)
        back[w] = (
            jnp.dot(fold[...], block, preferred_element_type=f32).astype(bf16).reshape(depth, slot_rows, fold_cols)
        )
        for dz in range(depth):
            src, dst = back.at[w, dz], returned.at[mine]
            returns[w, dz] = Local(src, dst) if (w, dz) == (0, 0) else send(src, dst, peer(w, -dz))

    g0, g1 = gathers
    enter(0)
    for h in (0, 1):
        g0.step1(h)
    for h in (0, 1):
        g0.onward(h, 0)
    for h in (0, 1):
        g0.step3(h)
    enter(1)
    for a in (3, 1):
        for h in (0, 1):
            g0.onward(h, a)
    for h in (0, 1):
        g1.step1(h)
    for h in (0, 1):
        g0.onward(h, 2)
    for h in (0, 1):
        g1.onward(h, 0)
    g0.end()
    loads[0].wait()
    up_piece(0, 0)
    for h in (0, 1):
        g1.step3(h)
    up_piece(0, 1)
    for h in (0, 1):
        g1.onward(h, 3)
    up_piece(0, 2)
    for h in (0, 1):
        g1.onward(h, 1)
    up_piece(0, 3)
    for h in (0, 1):
        g1.onward(h, 2)
    loads[1].wait()
    down_and_send(0)
    g1.end()
    up_piece(1, 0)
    for h in (0, 1):
        sums[0].s2(h, 0)
    up_piece(1, 1)
    for h in (0, 1):
        sums[0].s2(h, 1)
    up_piece(1, 2)
    up_piece(1, 3)
    for h in (0, 1):
        sums[0].s3(h)
    down_and_send(1)
    for h in (0, 1):
        sums[0].s5(h)
    for quarter in (0, 1):
        for h in (0, 1):
            sums[1].s2(h, quarter)
    leave(0)
    for h in (0, 1):
        sums[1].s3(h)
    for h in (0, 1):
        sums[1].s5(h)
    leave(1)
    for w in (0, 1):
        for dz in range(depth):
            returns[w, dz].wait_recv()
    block = returned[...].reshape(2 * depth * slot_rows, fold_cols)
    experts = jnp.dot(put[...], block, preferred_element_type=f32)
    for j in range(8):
        cols = slice(j * fold_cols, (j + 1) * fold_cols)
        out[:, cols] = (resid[:, cols] + gating * experts[j * 8 : j * 8 + 8]).astype(bf16)
    for copy in sent:
        copy.wait_send()
    assert count[0] <= NSEM


def per_device(
    residual_in, context, out_weight, norm_gain, router, up_weight, down_weight, modality, expert
):
    tok_rows, width = residual_in.shape
    depth = lax.axis_size("exp")
    hidden_units = up_weight.shape[3]
    fold_cols = width // 8
    slot_rows = CAP * depth
    routes = modality * EXPERTS + expert
    kinds = 2 * EXPERTS
    hot = routes[:, None] == jnp.arange(kinds, dtype=jnp.int32)[None, :]
    same = (routes[:, None] == routes[None, :]) & (
        jnp.arange(tok_rows)[:, None] > jnp.arange(tok_rows)[None, :]
    )
    target = routes * CAP + jnp.sum(same.astype(jnp.int32), axis=1)
    placed = (jnp.arange(kinds * CAP, dtype=jnp.int32)[:, None] == target[None, :]).astype(f32)
    eye = jnp.eye(8, dtype=f32)
    by_slot = placed.reshape(kinds, CAP, tok_rows)
    pick = jnp.einsum("mcq,ij->mcijq", by_slot, eye).reshape(kinds * CAP * 8, 8 * tok_rows).astype(bf16)
    halves = depth // EXPERTS
    put = jnp.broadcast_to(
        jnp.einsum("mcq,ij->iqmcj", by_slot, eye)[:, :, :, None],
        (8, tok_rows, kinds, halves, CAP, 8),
    ).reshape(8 * tok_rows, kinds * halves * CAP * 8).astype(bf16)
    n = 8 * slot_rows
    line = jnp.arange(n)
    source = (line % slot_rows) // CAP * (CAP * 8) + (line % CAP) * 8 + line // slot_rows
    unfold = (source[:, None] == line[None, :]).astype(bf16)
    fold = (source[None, :] == line[:, None]).astype(bf16)
    rows, group = context.shape[0], out_weight.shape[1]
    q = width // 4
    g4 = group // 4
    vm = pltpu.VMEM
    scratch = [
        vm((depth, 2, rows, context.shape[1]), bf16),
        vm((2 * rows, group), f32),
        vm((4, 4, rows, group), bf16),
        vm((4, 4, rows, g4), bf16),
        vm((2, 2, 4, rows, 2 * g4), bf16),
        vm((2, 4, rows, 2 * g4), bf16),
        vm((4, rows, g4), bf16),
        vm((2, 2, rows, 2 * g4), bf16),
        vm((2 * depth, 16, group // 2), bf16),
        vm((2 * depth, 16, group // 2), bf16),
        vm((tok_rows, width), f32),
        vm((8 * tok_rows, fold_cols), bf16),
        vm((kinds, CAP * 8, fold_cols), bf16),
        vm((2, depth, CAP * 8, fold_cols), bf16),
        vm((2, 4, 4, slot_rows, width), bf16),
        vm((width, hidden_units), bf16),
        vm((hidden_units, width), bf16),
        vm((16 * slot_rows, hidden_units), f32),
        vm((16 * slot_rows, hidden_units), bf16),
        vm((2, 4, 4, slot_rows, width), bf16),
        vm((2, 4, 4, slot_rows, q), bf16),
        vm((2, 2, 2, 4, slot_rows, 2 * q), bf16),
        vm((2, 2, 4, slot_rows, 2 * q), bf16),
        vm((2, 4, slot_rows, q), bf16),
        vm((2, 2, 2, slot_rows, 2 * q), bf16),
        vm((2, depth, CAP * 8, fold_cols), bf16),
        vm((2 * depth, CAP * 8, fold_cols), bf16),
        pltpu.SemaphoreType.DMA((NSEM,)),
        pltpu.SemaphoreType.DMA((NSEM,)),
        pltpu.SemaphoreType.DMA((2,)),
    ]
    local = pl.BlockSpec(memory_space=pltpu.VMEM)
    there = pl.BlockSpec(memory_space=pl.ANY)
    return pl.pallas_call(
        functools.partial(kernel, depth),
        out_shape=jax.ShapeDtypeStruct((tok_rows, width), bf16),
        in_specs=[local] * 10 + [there] * 2,
        out_specs=local,
        scratch_shapes=scratch,
        compiler_params=pltpu.CompilerParams(
            collective_id=0, has_side_effects=True, vmem_limit_bytes=63_000_000
        ),
    )(
        residual_in,
        context,
        out_weight,
        norm_gain.reshape(1, width),
        router.reshape(kinds, width),
        hot.astype(f32),
        pick,
        put,
        unfold,
        fold,
        up_weight.reshape(width, hidden_units),
        down_weight.reshape(hidden_units, width),
    )


def solution(mesh):
    in_specs = (
        P(("role", "exp", "tp"), None),
        P(("role", "exp"), "tp"),
        P("tp", ("role", "exp")),
        P(),
        P(),
        P("role", "exp", None, "tp"),
        P("role", "exp", "tp", None),
        P(("role", "exp", "tp")),
        P(("role", "exp", "tp")),
    )
    out_specs = P(("role", "exp", "tp"), None)
    return jax.shard_map(
        per_device, mesh=mesh, in_specs=in_specs, out_specs=out_specs, check_vma=False
    )
```

time: 413 us -> 184 us (0.45)
  waiting for transfers between devices: 323 us -> 0 us
  Pallas kernels: 0 us -> 173 us
  matrix products: 27.7 us -> 0 us
  starting transfers between devices: 20.1 us -> 0 us
  blocking collectives: 19.5 us -> 0 us
  between operations: 13.2 us -> 0.05 us
  local copies, waits for them, and re-layouts: 2.9 us -> 7.67 us
    pallas_call x0 -> x1, Pallas kernels: none -> 173 us  [per_device(): pl.pallas_call(functools.partial(kernel, depth), out_shape=jax.ShapeDtype...]
    all_gather x2 -> x0, waiting for transfers between devices: 128 us -> none  [the longest x1 82 us: per_device(): lax.all_gather(local_slots, 'tp', axis=0, tiled=True)]
    reduce_scatter x1 -> x0, waiting for transfers between devices: 116 us -> none  [per_device(): lax.psum_scatter(jnp.dot(hidden, down_matrix, preferred_element_type=jnp....]
    all_to_all x3 -> x0, waiting for transfers between devices: 79.3 us -> none  [the longest x1 55.5 us: summed_on_arrival(): lax.all_to_all(in_blocks(array, dim, length), axis, 0, 0, tiled=True)]
    dot_general x6 -> x0, matrix products: 27.7 us -> none  [the longest x1 10.9 us: per_device(): jnp.dot(hidden, down_matrix, preferred_element_type=jnp.float32)]
    all_to_all x3 -> x0, starting transfers between devices: 20 us -> none  [the longest x1 8.01 us: joined_exchange(): lax.all_to_all(blocks, axis, split_axis=0, concat_axis=0, tiled=True)]
    all_to_all x1 -> x0, blocking collectives: 19.5 us -> none  [joined_exchange(): lax.all_to_all(blocks, axis, split_axis=0, concat_axis=0, tiled=True)]
  transfers between devices with their start and end apart: 6 -> 0, of which waited for: 6 -> 0; matrix products, arithmetic and copies ran while one was open for 0% -> 0% of each run, Pallas kernels for 0% -> 0%
where the time goes in v1:
time: 184 us; the launch traced here: 183 us
  Pallas kernels  173 us (94%)
  local copies, waits for them, and re-layouts  7.67 us (4%)
  other arithmetic  2.78 us (2%)
    pallas_call x1, Pallas kernels, per_device(): pl.pallas_call(functools.partial(kernel, depth), out_shape=jax.ShapeDtype...  173 us

profile of v1, /device:TPU:1, one launch (start us, length us, event | category | flops | bytes accessed | tf_op | source)
XLA Modules:
  0.0 183.4 jit_solution(9147713022663626782)
XLA Ops:
  0.0 1.3 reshape.127.gain
  1.3 1.6 reshape.128.router
  2.9 0.7 multiply_add_fusion.2
  3.6 0.7 fusion.4.mask
  4.3 0.2 convert_reduce_fusion
  4.5 0.1 compare_convert_fusion
  4.6 0.5 fusion
  5.0 0.2 convert_element_type.30
  5.3 0.7 copy.12.pick
  6.0 0.7 copy.11
  6.7 0.3 broadcast_in_dim.2
  6.9 1.3 convert_element_type.32.put
  8.2 0.7 fusion.3
  8.9 172.9 %shard_map.91 = bf16[8,8192]{1,0:T(8,128)(2,1)} custom-call(bf16[8,8192]{1,0:T(8,128)(2,1)} %residual.1, bf16[128,512]{1,0:T(8,128)(2,1)} %context.1, bf16[512,512]{1,0:T(8,128)(2,1)} %out_weight.1, bf16[1,8192]{1,0:T(2,128)(2,1)} %reshape.127.gain, bf16[8,8192]{1,0:T(8,128)(2,1)} %reshape.128.router, f32[8,8]{1,0:T(8,128)} %fusion.4.mask, ...), custom_call_target="tpu_custom_call" | custom-call | tf_op jit(solution)/shard_map/pallas_call | solution.py:514
  181.8 1.6 copy.14
  (4 shorter events, 0.0 us)

commit v2 on v1

--- a/solution.py
+++ b/solution.py
@@ -11,7 +11,7 @@
 CAP = 2
 EPSILON = 1e-05
 SIDE = 4
-NSEM = 224
+NSEM = 256
 f32, bf16 = jnp.float32, jnp.bfloat16
 MESH = pl.DeviceIdType.MESH
 
@@ -153,9 +153,9 @@
 
 
 def kernel(
-    depth, residual, context, out_weight, gain, router, mask, pick, put, unfold, fold, up_hbm, down_hbm, out,
-    cg, res, p1, p1q, p1f, p1s, p1q2, p1f2, tiles, heads, resid, folded, outgoing, arrived,
-    grid, up, down, acc, hidden, part, rq, rf, rs, rq2, rf2, back, returned, ssem, rsem, wsem,
+    depth, modality, expert, residual_in, context, out_weight_in, gain_in, router_in, up_hbm, down_hbm, out,
+    residual, out_weight, gain, router, pick, put, unfold, fold, cg, res, wave_a, wave_b, tiles, heads, resid, folded,
+    outgoing, arrived, grid, up, down, acc, hidden, part, rq, rf, rs, rq2, rf2, back, returned, ssem, rsem, wsem,
 ):
     r, z, t = lax.axis_index("role"), lax.axis_index("exp"), lax.axis_index("tp")
     x, y = t // SIDE, t % SIDE
@@ -192,28 +192,75 @@
     def peer(dr, dz):
         return (lax.rem(r + dr, 2), lax.rem(z + dz + depth, depth), t)
 
-    loads = [pltpu.make_async_copy(up_hbm, up, wsem.at[0]), pltpu.make_async_copy(down_hbm, down, wsem.at[1])]
-    for load in loads:
-        load.start()
-
+    mid = depth // 2
     barrier = pltpu.get_barrier_semaphore()
     others = [peer(dr, dz) for dz in range(depth) for dr in (0, 1) if (dr, dz) != (0, 0)]
     others += [near(axis, step) for axis in (0, 1) for step in (1, -1)]
     for device in others:
         pl.semaphore_signal(barrier, inc=1, device_id=device, device_id_type=MESH)
+    pairs = [(context, cg.at[0, 0]), (out_weight_in, out_weight), (residual_in, residual), (gain_in, gain),
+             (router_in, router), (up_hbm, up), (down_hbm, down)]
+    loads = [pltpu.make_async_copy(src, dst, wsem.at[i]) for i, (src, dst) in enumerate(pairs)]
+    for load in loads:
+        load.start()
+
+    routes = [modality[i] * EXPERTS + expert[i] for i in range(8)]
+    slot_of = []
+    for i in range(8):
+        place = routes[i] * CAP
+        for k in range(i):
+            place = place + jnp.where(routes[k] == routes[i], 1, 0)
+        slot_of.append(place)
+
+    def spread(values, index):
+        total = jnp.zeros(index.shape, jnp.int32)
+        for i, value in enumerate(values):
+            total = jnp.where(index == i, value, total)
+        return total
+
+    def table(shape):
+        return (lax.broadcasted_iota(jnp.int32, shape, 0), lax.broadcasted_iota(jnp.int32, shape, 1))
+
+    row, col = table(pick.shape)
+    pick[...] = jnp.where(((row >> 3) == spread(slot_of, col & 7)) & ((row & 7) == (col >> 3)), 1.0, 0.0).astype(bf16)
+    row, col = table(put.shape)
+    slot = (col >> 5) * 2 + ((col >> 3) & 1)
+    put[...] = jnp.where((slot == spread(slot_of, row & 7)) & ((col & 7) == (row >> 3)), 1.0, 0.0).astype(bf16)
+    row, col = table(unfold.shape)
+    unfold[...] = jnp.where(((row & 15) >> 1) * 16 + (row & 1) * 8 + (row >> 4) == col, 1.0, 0.0).astype(bf16)
+    fold[...] = jnp.where(((col & 15) >> 1) * 16 + (col & 1) * 8 + (col >> 4) == row, 1.0, 0.0).astype(bf16)
+    row, col = table((8, 1))
+    route_rows = spread(routes, row)
+    loads[0].wait()
     pl.semaphore_wait(barrier, len(others))
 
-    rows = context.shape[0]
-    mid = depth // 2
-    partner = peer(1, 0)
-    up_z, down_z = peer(0, 1), peer(0, -1)
-    shared = {0: send(context, cg.at[0, 1], partner)}
-    going = send(context, cg.at[depth - 1, 0], up_z)
-    coming = send(context, cg.at[1, 0], down_z)
-
-    def project(dz, own):
-        shared[dz].wait_recv()
-        both = jnp.concatenate([own, cg[dz, 1]], axis=0)
+    rows = cg.shape[2]
+    half_rows = rows // 2
+    partner, up_z, down_z = peer(1, 0), peer(0, 1), peer(0, -1)
+    piece = [pl.ds(0, half_rows), pl.ds(half_rows, half_rows)]
+
+    def pass_on(a, b, c, device):
+        return send(cg.at[a, 0, piece[c]], cg.at[b, 0, piece[c]], device)
+
+    def hand_over(a, c):
+        return send(cg.at[a, 0, piece[c]], cg.at[a, 1, piece[c]], partner)
+
+    going = {0: pass_on(0, depth - 1, 0, up_z)}
+    coming = {0: pass_on(0, 1, 0, down_z)}
+    shared = {0: [send(cg.at[0, 0], cg.at[0, 1], partner)]}
+    going[1] = pass_on(0, depth - 1, 1, up_z)
+    coming[1] = pass_on(0, 1, 1, down_z)
+    loads[1].wait()
+
+    order = [0, 1, depth - 1, 2, depth - 2, 3, depth - 3, mid]
+    first = 5
+
+    def project(dz):
+        for copy in shared[dz]:
+            copy.wait_recv()
+        at_wave = order.index(dz)
+        p1, low = (wave_a[0], at_wave * 16) if at_wave < first else (wave_b[0], (at_wave - first) * 16)
+        both = jnp.concatenate([cg[dz, 0], cg[dz, 1]], axis=0)
         res[...] = jnp.dot(both, out_weight[...], preferred_element_type=f32)
 
         def body(i, _):
@@ -221,81 +268,107 @@
             home = lax.rem(x + dx, SIDE) * SIDE + lax.rem(y + dy, SIDE)
             at = pl.multiple_of(home * 8, 8)
             block = jnp.concatenate([res[pl.ds(at, 8), :], res[pl.ds(rows + at, 8), :]], axis=0)
-            p1[dx, dy, pl.ds(dz * 16, 16), :] = block.astype(bf16)
+            p1[dx, dy, pl.ds(low, 16), :] = block.astype(bf16)
             return 0
 
         lax.fori_loop(0, SIDE * SIDE, body, 0)
 
-    half_rows = rows // 2
-    pending = [0]
-    for step in range(1, mid):
+    def ring_step(step):
+        nonlocal going, coming
         a, b = depth - step, step
-        going.wait_recv()
-        if step < mid - 1:
-            going_next = send(cg.at[a, 0], cg.at[a - 1, 0], up_z)
-        else:
-            going_next = send(cg.at[a, 0, pl.ds(0, half_rows)], cg.at[mid, 0, pl.ds(0, half_rows)], up_z)
-        shared[a] = send(cg.at[a, 0], cg.at[a, 1], partner)
-        coming.wait_recv()
-        if step < mid - 1:
-            coming_next = send(cg.at[b, 0], cg.at[b + 1, 0], down_z)
-        else:
-            coming_next = send(cg.at[b, 0, pl.ds(half_rows, half_rows)], cg.at[mid, 0, pl.ds(half_rows, half_rows)], down_z)
-        shared[b] = send(cg.at[b, 0], cg.at[b, 1], partner)
+        shared[a], shared[b] = [], []
+        going_next, coming_next = {}, {}
+        for c in (0, 1):
+            going[c].wait_recv()
+            if step < mid - 1 or c == 0:
+                going_next[c] = pass_on(a, a - 1, c, up_z)
+            coming[c].wait_recv()
+            if step < mid - 1 or c == 1:
+                coming_next[c] = pass_on(b, b + 1, c, down_z)
+            shared[a].append(hand_over(a, c))
+            shared[b].append(hand_over(b, c))
         going, coming = going_next, coming_next
-        for dz in pending:
-            project(dz, context[...] if dz == 0 else cg[dz, 0])
-        pending = [a, b]
-    going.wait_recv()
-    coming.wait_recv()
-    shared[mid] = send(cg.at[mid, 0], cg.at[mid, 1], partner)
-    for dz in pending + [mid]:
-        project(dz, cg[dz, 0])
-
-    heads_sum = Sums(send, near, p1, p1q, p1f, p1s, p1q2, p1f2)
-    for quarter in (0, 1):
-        for h in (0, 1):
-            heads_sum.s1(h, quarter)
-    for quarter in (0, 1):
-        for h in (0, 1):
-            heads_sum.s2(h, quarter)
-    for h in (0, 1):
-        heads_sum.s3(h)
-    for h in (0, 1):
-        heads_sum.s5(h)
-    final = [heads_sum.s6(h) for h in (0, 1)]
-    for i in range(2 * depth):
-        tiles[i] = jnp.concatenate([final[0][8 * i : 8 * i + 8], final[1][8 * i : 8 * i + 8]], axis=0).astype(bf16)
-
+
+    sum_a, sum_b = Sums(send, near, *wave_a), Sums(send, near, *wave_b)
+    both_halves = (0, 1)
+
+    def each(step, *rest):
+        for args in rest or ((),):
+            for h in both_halves:
+                step(h, *args)
+
+    ring_step(1)
+    project(0)
+    ring_step(2)
+    project(depth - 1)
+    project(1)
+    ring_step(3)
+    project(depth - 2)
+    project(2)
+    each(sum_a.s1, (0,), (1,))
+    going[0].wait_recv()
+    shared[mid] = [hand_over(mid, 0)]
+    coming[1].wait_recv()
+    shared[mid].append(hand_over(mid, 1))
+    project(depth - 3)
+    project(3)
+    each(sum_a.s2, (0,))
+    project(mid)
+    each(sum_b.s1, (0,), (1,))
+    each(sum_a.s2, (1,))
+    each(sum_a.s3)
+    each(sum_b.s2, (0,), (1,))
+    each(sum_a.s5)
+    each(sum_b.s3)
     mine = r * depth + z
-    columns = []
-    for dz in range(depth):
-        for dr in (0, 1):
-            src, dst = tiles.at[dz * 2 + dr], heads.at[mine]
-            columns.append(Local(src, dst) if (dr, dz) == (0, 0) else send(src, dst, peer(dr, dz)))
-    for copy in columns:
-        copy.wait_recv()
+    columns = {}
+
+    def to_tokens(total, dzs):
+        final = [total.s6(h) for h in both_halves]
+        for i, dz in enumerate(dzs):
+            for dr in (0, 1):
+                at = slice(i * 16 + dr * 8, i * 16 + dr * 8 + 8)
+                tiles[dz * 2 + dr] = jnp.concatenate([final[0][at], final[1][at]], axis=0).astype(bf16)
+        for dz in dzs:
+            for dr in (0, 1):
+                src, dst = tiles.at[dz * 2 + dr], heads.at[mine]
+                columns[dr, dz] = Local(src, dst) if (dr, dz) == (0, 0) else send(src, dst, peer(dr, dz))
+
+    to_tokens(sum_a, order[:first])
+    each(sum_b.s5)
+    to_tokens(sum_b, order[first:])
+    for load in loads[2:5]:
+        load.wait()
+
     group = width // (2 * depth)
     squares = jnp.zeros((8, group), f32)
-    for g in range(2 * depth):
-        block = heads[g].astype(f32)
-        whole = jnp.concatenate([block[:8], block[8:]], axis=1)
-        cols = slice(g * group, (g + 1) * group)
-        value = (residual[:, cols].astype(f32) + whole).astype(bf16).astype(f32)
-        resid[:, cols] = value
-        squares = squares + value * value
+    for dz in order:
+        for dr in (0, 1):
+            columns[dr, dz].wait_recv()
+            source = lax.rem(r + dr, 2) * depth + lax.rem(z - dz + depth, depth)
+            block = heads[source].astype(f32)
+            whole = jnp.concatenate([block[:8], block[8:]], axis=1)
+            cols = pl.ds(pl.multiple_of(source * group, group), group)
+            value = (residual[:, cols].astype(f32) + whole).astype(bf16).astype(f32)
+            resid[:, cols] = value
+            squares = squares + value * value
     inverse = lax.rsqrt(jnp.sum(squares, axis=1, keepdims=True) / width + EPSILON)
     logits = jnp.zeros((8, fold_cols), f32)
-    choice = mask[...]
+    lanes = gain.shape[1]
+    per_fold = fold_cols // lanes
     for j in range(0, 8, 2):
         pair = []
         for i in (j, j + 1):
             cols = slice(i * fold_cols, (i + 1) * fold_cols)
-            normed = (resid[:, cols] * inverse * gain[:, cols].astype(f32)).astype(bf16).astype(f32)
-            rows_of = router[:, cols].astype(f32)
-            picked = choice[:, 0:1] * rows_of[0:1]
-            for e in range(1, 2 * EXPERTS):
-                picked = picked + choice[:, e : e + 1] * rows_of[e : e + 1]
+            gains = gain[pl.ds(i * per_fold, per_fold), :].astype(f32)
+            gains = jnp.concatenate(
+                [jnp.broadcast_to(gains[k : k + 1], (8, lanes)) for k in range(per_fold)], axis=1
+            )
+            normed = (resid[:, cols] * inverse * gains).astype(bf16).astype(f32)
+            picked = jnp.zeros((8, fold_cols), f32)
+            for e in range(2 * EXPERTS):
+                line = router[e // EXPERTS, :, cols].astype(f32)[e % EXPERTS : e % EXPERTS + 1]
+                picked = jnp.where(route_rows == e, line, picked)
             logits = logits + normed * picked
             pair.append(normed)
         folded[pl.ds(j * 8, 16), :] = jnp.concatenate(pair, axis=0).astype(bf16)
@@ -393,7 +466,7 @@
     for h in (0, 1):
         g1.onward(h, 0)
     g0.end()
-    loads[0].wait()
+    loads[5].wait()
     up_piece(0, 0)
     for h in (0, 1):
         g1.step3(h)
@@ -406,7 +479,7 @@
     up_piece(0, 3)
     for h in (0, 1):
         g1.onward(h, 2)
-    loads[1].wait()
+    loads[6].wait()
     down_and_send(0)
     g1.end()
     up_piece(1, 0)
@@ -452,40 +525,35 @@
     hidden_units = up_weight.shape[3]
     fold_cols = width // 8
     slot_rows = CAP * depth
-    routes = modality * EXPERTS + expert
     kinds = 2 * EXPERTS
-    hot = routes[:, None] == jnp.arange(kinds, dtype=jnp.int32)[None, :]
-    same = (routes[:, None] == routes[None, :]) & (
-        jnp.arange(tok_rows)[:, None] > jnp.arange(tok_rows)[None, :]
-    )
-    target = routes * CAP + jnp.sum(same.astype(jnp.int32), axis=1)
-    placed = (jnp.arange(kinds * CAP, dtype=jnp.int32)[:, None] == target[None, :]).astype(f32)
-    eye = jnp.eye(8, dtype=f32)
-    by_slot = placed.reshape(kinds, CAP, tok_rows)
-    pick = jnp.einsum("mcq,ij->mcijq", by_slot, eye).reshape(kinds * CAP * 8, 8 * tok_rows).astype(bf16)
-    halves = depth // EXPERTS
-    put = jnp.broadcast_to(
-        jnp.einsum("mcq,ij->iqmcj", by_slot, eye)[:, :, :, None],
-        (8, tok_rows, kinds, halves, CAP, 8),
-    ).reshape(8 * tok_rows, kinds * halves * CAP * 8).astype(bf16)
-    n = 8 * slot_rows
-    line = jnp.arange(n)
-    source = (line % slot_rows) // CAP * (CAP * 8) + (line % CAP) * 8 + line // slot_rows
-    unfold = (source[:, None] == line[None, :]).astype(bf16)
-    fold = (source[None, :] == line[:, None]).astype(bf16)
     rows, group = context.shape[0], out_weight.shape[1]
     q = width // 4
     g4 = group // 4
     vm = pltpu.VMEM
+
+    def sum_buffers(lines):
+        return [
+            vm((4, 4, lines, group), bf16),
+            vm((4, 4, lines, g4), bf16),
+            vm((2, 2, 4, lines, 2 * g4), bf16),
+            vm((2, 4, lines, 2 * g4), bf16),
+            vm((4, lines, g4), bf16),
+            vm((2, 2, lines, 2 * g4), bf16),
+        ]
+
     scratch = [
+        vm((tok_rows, width), bf16),
+        vm(out_weight.shape, bf16),
+        vm((width // 128, 128), bf16),
+        vm(router.shape, bf16),
+        vm((kinds * CAP * 8, 8 * tok_rows), bf16),
+        vm((8 * tok_rows, 2 * depth * CAP * 8), bf16),
+        vm((8 * slot_rows, 8 * slot_rows), bf16),
+        vm((8 * slot_rows, 8 * slot_rows), bf16),
         vm((depth, 2, rows, context.shape[1]), bf16),
         vm((2 * rows, group), f32),
-        vm((4, 4, rows, group), bf16),
-        vm((4, 4, rows, g4), bf16),
-        vm((2, 2, 4, rows, 2 * g4), bf16),
-        vm((2, 4, rows, 2 * g4), bf16),
-        vm((4, rows, g4), bf16),
-        vm((2, 2, rows, 2 * g4), bf16),
+        sum_buffers(80),
+        sum_buffers(48),
         vm((2 * depth, 16, group // 2), bf16),
         vm((2 * depth, 16, group // 2), bf16),
         vm((tok_rows, width), f32),
@@ -507,30 +575,27 @@
         vm((2 * depth, CAP * 8, fold_cols), bf16),
         pltpu.SemaphoreType.DMA((NSEM,)),
         pltpu.SemaphoreType.DMA((NSEM,)),
-        pltpu.SemaphoreType.DMA((2,)),
+        pltpu.SemaphoreType.DMA((7,)),
     ]
     local = pl.BlockSpec(memory_space=pltpu.VMEM)
     there = pl.BlockSpec(memory_space=pl.ANY)
     return pl.pallas_call(
         functools.partial(kernel, depth),
         out_shape=jax.ShapeDtypeStruct((tok_rows, width), bf16),
-        in_specs=[local] * 10 + [there] * 2,
+        in_specs=[pl.BlockSpec(memory_space=pltpu.SMEM)] * 2 + [there] * 7,
         out_specs=local,
         scratch_shapes=scratch,
         compiler_params=pltpu.CompilerParams(
             collective_id=0, has_side_effects=True, vmem_limit_bytes=63_000_000
         ),
     )(
+        modality,
+        expert,
         residual_in,
         context,
         out_weight,
-        norm_gain.reshape(1, width),
-        router.reshape(kinds, width),
-        hot.astype(f32),
-        pick,
-        put,
-        unfold,
-        fold,
+        norm_gain.reshape(width // 128, 128),
+        router,
         up_weight.reshape(width, hidden_units),
         down_weight.reshape(hidden_units, width),
     )

time: 184 us -> 171 us (0.929)
  local copies, waits for them, and re-layouts: 7.67 us -> 1.57 us
  Pallas kernels: 173 us -> 169 us
  other arithmetic: 2.78 us -> 0 us
    pallas_call x1, Pallas kernels: 173 us -> 169 us  [per_device(): pl.pallas_call(functools.partial(kernel, depth), out_shape=jax.ShapeDtype...]
    reshape x2 -> x0, local copies, waits for them, and re-layouts: 2.93 us -> none  [the longest x1 1.59 us: per_device(): router.reshape(kinds, width)]
    convert_element_type x4 -> x0, local copies, waits for them, and re-layouts: 2.9 us -> none  [the longest x2 1.93 us: per_device(): put = jnp.broadcast_to(jnp.einsum('mcq,ij->iqmcj', by_slot, eye)[:, :, :,...]
where the time goes in v2:
time: 171 us; the launch traced here: 170 us
  Pallas kernels  169 us (99%)
    pallas_call x1, Pallas kernels, per_device(): pl.pallas_call(functools.partial(kernel, depth), out_shape=jax.ShapeDtype...  169 us

profile of v2, /device:TPU:1, one launch (start us, length us, event | category | flops | bytes accessed | tf_op | source)
XLA Modules:
  0.0 170.3 jit_solution(3566754450361588770)
XLA Ops:
  0.0 168.7 %shard_map.91 = bf16[8,8192]{1,0:T(8,128)(2,1)} custom-call(s32[8]{0:T(128)} %modality.1, s32[8]{0:T(128)} %expert.1, bf16[8,8192]{1,0:T(8,128)(2,1)} %residual_in.1, bf16[128,512]{1,0:T(8,128)(2,1)} %context.1, bf16[512,512]{1,0:T(8,128)(2,1)} %out_weight_in.1, bf16[64,128]{1,0:T(8,128)(2,1)} %bitcast.5, bf16[2,4,8192]{2,1,0:T(4,128)(2,1)} %router_in.1, ...), custom_call_target="tpu_custom_call" | custom-call | tf_op jit(solution)/shard_map/pallas_call | solution.py:582
  168.8 1.6 copy.11

commit v3 on v2

--- a/solution.py
+++ b/solution.py
@@ -11,105 +11,121 @@
 CAP = 2
 EPSILON = 1e-05
 SIDE = 4
-NSEM = 256
+NSEM = 320
 f32, bf16 = jnp.float32, jnp.bfloat16
 MESH = pl.DeviceIdType.MESH
 
 
 class Sums:
-    def __init__(self, send, near, src, q, f, s, q2, f2):
-        self.send, self.near = send, near
+    def __init__(self, send, near, src, q, f, s, q2, f2, side=None, arrivals=None):
+        self.send, self.near, self.side, self.arrivals = send, near, side, arrivals
         self.src, self.q, self.f, self.s, self.q2, self.f2 = src, q, f, s, q2, f2
-        self.width = src.shape[3]
-        self.part = self.width // 4
         self.m, self.n = {}, {}
 
-    def sel(self, h, k, c, w):
-        cols = pl.ds(c, w)
-        return self.src.at[:, k, :, cols] if h == 0 else self.src.at[k, :, :, cols]
-
-    def base(self, h):
-        return h * 2 * self.part
+    def sel(self, h, k, quarter):
+        at = 2 * h + quarter
+        return self.src.at[at, :, k] if h == 0 else self.src.at[at, k]
+
+    def add_side(self, h, quarter, *ks):
+        if self.side is None or (h, quarter) != (0, 0):
+            return
+        cols = pl.ds(0, self.side.shape[3])
+        for k in ks:
+            self.arrivals[k].wait_recv()
+
+            def body(i, _, k=k):
+                was = self.src[0, i, k, :, cols].astype(f32)
+                self.src[0, i, k, :, cols] = (was + self.side[k, i].astype(f32)).astype(bf16)
+                return 0
+
+            lax.fori_loop(0, SIDE, body, 0)
 
     def s1(self, h, quarter):
-        p, a = self.part, self.base(h)
+        self.add_side(h, quarter, 2, 3)
         plus, minus = self.near(1 - h, 1), self.near(1 - h, -1)
         if quarter == 0:
-            self.m[h, 1] = self.send(self.sel(h, 2, a, p), self.q.at[h * 2], plus)
-            self.m[h, 4] = self.send(self.sel(h, 3, a, p), self.f.at[h, 1, :, :, pl.ds(0, p)], minus)
+            self.m[h, 1] = self.send(self.sel(h, 2, 0), self.q.at[h * 2], plus)
+            self.m[h, 4] = self.send(self.sel(h, 3, 0), self.f.at[h, 1, 0], minus)
         else:
-            self.m[h, 2] = self.send(self.sel(h, 2, a + p, p), self.q.at[h * 2 + 1], minus)
-            self.m[h, 3] = self.send(self.sel(h, 1, a + p, p), self.f.at[h, 0, :, :, pl.ds(p, p)], plus)
+            self.m[h, 2] = self.send(self.sel(h, 2, 1), self.q.at[h * 2 + 1], minus)
+            self.m[h, 3] = self.send(self.sel(h, 1, 1), self.f.at[h, 0, 1], plus)
 
     def s2(self, h, quarter):
-        p, a = self.part, self.base(h)
-        k, c, which = (1, a, 1) if quarter == 0 else (3, a + p, 2)
-        got = self.q.at[h * 2 + quarter]
+        k, which = (1, 1) if quarter == 0 else (3, 2)
+        at = 2 * h + quarter
+        got = self.q.at[at]
+        self.add_side(h, quarter, 1)
         self.m[h, which].wait_recv()
-        cols = pl.ds(c, p)
 
         def body(i, _):
-            at = (i, k, slice(None), cols) if h == 0 else (k, i, slice(None), cols)
-            self.src[at] = (self.src[at].astype(f32) + got[i].astype(f32)).astype(bf16)
+            where = (at, i, k) if h == 0 else (at, k, i)
+            self.src[where] = (self.src[where].astype(f32) + got[i].astype(f32)).astype(bf16)
             return 0
 
         lax.fori_loop(0, SIDE, body, 0)
         if quarter == 0:
-            self.m[h, 5] = self.send(self.sel(h, 1, c, p), self.f.at[h, 0, :, :, pl.ds(0, p)], self.near(1 - h, 1))
+            self.m[h, 5] = self.send(self.sel(h, 1, 0), self.f.at[h, 0, 0], self.near(1 - h, 1))
         else:
-            self.m[h, 6] = self.send(self.sel(h, 3, c, p), self.f.at[h, 1, :, :, pl.ds(p, p)], self.near(1 - h, -1))
+            self.m[h, 6] = self.send(self.sel(h, 3, 1), self.f.at[h, 1, 1], self.near(1 - h, -1))
 
     def s3(self, h):
+        self.add_side(h, 0, 0)
         for i in (3, 4, 5, 6):
             self.m[h, i].wait_recv()
-        p = self.part
-        cols = pl.ds(self.base(h), 2 * p)
 
         def body(i, _):
-            at = (i, 0, slice(None), cols) if h == 0 else (0, i, slice(None), cols)
-            total = self.src[at].astype(f32) + self.f[h, 0, i].astype(f32) + self.f[h, 1, i].astype(f32)
-            self.s[h, i] = total.astype(bf16)
+            for quarter in (0, 1):
+                at = 2 * h + quarter
+                where = (at, i, 0) if h == 0 else (at, 0, i)
+                total = self.src[where].astype(f32) + self.f[h, 0, quarter, i].astype(f32)
+                self.s[h, quarter, i] = (total + self.f[h, 1, quarter, i].astype(f32)).astype(bf16)
             return 0
 
         lax.fori_loop(0, SIDE, body, 0)
         plus, minus = self.near(h, 1), self.near(h, -1)
-        lo, hi = pl.ds(0, p), pl.ds(p, p)
-        self.n[h, 1] = self.send(self.s.at[h, 2, :, lo], self.q2.at[h * 2], plus)
-        self.n[h, 2] = self.send(self.s.at[h, 2, :, hi], self.q2.at[h * 2 + 1], minus)
-        self.n[h, 3] = self.send(self.s.at[h, 1, :, hi], self.f2.at[h, 0, :, hi], plus)
-        self.n[h, 4] = self.send(self.s.at[h, 3, :, lo], self.f2.at[h, 1, :, lo], minus)
+        self.n[h, 1] = self.send(self.s.at[h, 0, 2], self.q2.at[h * 2], plus)
+        self.n[h, 2] = self.send(self.s.at[h, 1, 2], self.q2.at[h * 2 + 1], minus)
+        self.n[h, 3] = self.send(self.s.at[h, 1, 1], self.f2.at[h, 0, 1], plus)
+        self.n[h, 4] = self.send(self.s.at[h, 0, 3], self.f2.at[h, 1, 0], minus)
 
     def s5(self, h):
-        p = self.part
-        lo, hi = pl.ds(0, p), pl.ds(p, p)
         self.n[h, 1].wait_recv()
-        self.s[h, 1, :, lo] = (self.s[h, 1, :, lo].astype(f32) + self.q2[h * 2].astype(f32)).astype(bf16)
-        self.n[h, 5] = self.send(self.s.at[h, 1, :, lo], self.f2.at[h, 0, :, lo], self.near(h, 1))
+        self.s[h, 0, 1] = (self.s[h, 0, 1].astype(f32) + self.q2[h * 2].astype(f32)).astype(bf16)
+        self.n[h, 5] = self.send(self.s.at[h, 0, 1], self.f2.at[h, 0, 0], self.near(h, 1))
         self.n[h, 2].wait_recv()
-        self.s[h, 3, :, hi] = (self.s[h, 3, :, hi].astype(f32) + self.q2[h * 2 + 1].astype(f32)).astype(bf16)
-        self.n[h, 6] = self.send(self.s.at[h, 3, :, hi], self.f2.at[h, 1, :, hi], self.near(h, -1))
+        self.s[h, 1, 3] = (self.s[h, 1, 3].astype(f32) + self.q2[h * 2 + 1].astype(f32)).astype(bf16)
+        self.n[h, 6] = self.send(self.s.at[h, 1, 3], self.f2.at[h, 1, 1], self.near(h, -1))
 
     def s6(self, h):
         for i in (3, 4, 5, 6):
             self.n[h, i].wait_recv()
-        return self.s[h, 0].astype(f32) + self.f2[h, 0].astype(f32) + self.f2[h, 1].astype(f32)
+        parts = []
+        for quarter in (0, 1):
+            total = self.s[h, quarter, 0].astype(f32) + self.f2[h, 0, quarter].astype(f32)
+            parts.append(total + self.f2[h, 1, quarter].astype(f32))
+        return jnp.concatenate(parts, axis=1)
 
 
 class Gather:
-    def __init__(self, send, near, dst):
-        self.send, self.near, self.dst = send, near, dst
-        self.part = dst.shape[3] // 4
+    def __init__(self, send, near, dst, base, twin):
+        self.send, self.near, self.dst, self.base, self.twin = send, near, dst, base, twin
+        self.part = (dst.shape[3] - base) // 4
         self.m = {}
 
     def blk(self, h, a, b, c, w):
         i, j = (a, b) if h == 0 else (b, a)
-        return self.dst.at[i, j, :, pl.ds(h * 2 * self.part + c, w)]
+        return self.dst.at[i, j, :, pl.ds(self.base + h * 2 * self.part + c, w)]
 
     def first(self, h, name, a, b, c, w, sign, a2):
         self.m[h, name] = self.send(self.blk(h, a, b, c, w), self.blk(h, a2, b, c, w), self.near(h, sign))
 
     def second(self, h, name, a, b, c, w, sign, b2):
         self.m[h, name] = self.send(self.blk(h, a, b, c, w), self.blk(h, a, b2, c, w), self.near(1 - h, sign))
+
+    def over(self, h, a, b):
+        if h == 0:
+            near, far = self.dst.at[a, b, :, pl.ds(self.base, self.base)], self.dst.at[a, b, :, pl.ds(0, self.base)]
+            self.m["z", a, b] = self.send(near, far, self.twin)
 
     def across(self, h, a):
         p = self.part
@@ -132,6 +148,8 @@
         self.first(h, "mm", 1, 0, p, p, -1, 2)
         self.across(h, 3)
         self.across(h, 1)
+        self.over(h, 3, 0)
+        self.over(h, 1, 0)
 
     def onward(self, h, a):
         p = self.part
@@ -139,23 +157,32 @@
         self.second(h, ("pp", a), a, 3, 0, p, 1, 2)
         self.m[h, ("m", a)].wait_recv()
         self.second(h, ("mm", a), a, 1, p, p, -1, 2)
+        self.over(h, a, 3)
+        self.over(h, a, 1)
 
     def step3(self, h):
         self.m[h, "pp"].wait_recv()
         self.m[h, "mm"].wait_recv()
         self.across(h, 2)
+        self.over(h, 2, 0)
+
+    def last(self, a):
+        for h in (0, 1):
+            self.m[h, ("pp", a)].wait_recv()
+            self.m[h, ("mm", a)].wait_recv()
+            self.over(h, a, 2)
 
     def end(self):
-        for h in (0, 1):
-            for a in range(SIDE):
-                self.m[h, ("pp", a)].wait_recv()
-                self.m[h, ("mm", a)].wait_recv()
+        for a in range(SIDE):
+            for b in range(SIDE):
+                if (a, b) != (0, 0):
+                    self.m["z", a, b].wait_recv()
 
 
 def kernel(
     depth, modality, expert, residual_in, context, out_weight_in, gain_in, router_in, up_hbm, down_hbm, out,
-    residual, out_weight, gain, router, pick, put, unfold, fold, cg, res, wave_a, wave_b, tiles, heads, resid, folded,
-    outgoing, arrived, grid, up, down, acc, hidden, part, rq, rf, rs, rq2, rf2, back, returned, ssem, rsem, wsem,
+    residual, out_weight, gain, router, pick, put, unfold, fold, cg, res, wave_bufs, tiles, heads, resid, folded,
+    outgoing, arrived, grid, up, down, acc, hidden, part, side_out, side_in, rq, rf, rs, rq2, rf2, back, returned, ssem, rsem, wsem,
 ):
     r, z, t = lax.axis_index("role"), lax.axis_index("exp"), lax.axis_index("tp")
     x, y = t // SIDE, t % SIDE
@@ -193,13 +220,20 @@
         return (lax.rem(r + dr, 2), lax.rem(z + dz + depth, depth), t)
 
     mid = depth // 2
+    parity = lax.rem(z, 2)
+    twin = (r, z + 1 - 2 * parity, t)
     barrier = pltpu.get_barrier_semaphore()
     others = [peer(dr, dz) for dz in range(depth) for dr in (0, 1) if (dr, dz) != (0, 0)]
     others += [near(axis, step) for axis in (0, 1) for step in (1, -1)]
     for device in others:
         pl.semaphore_signal(barrier, inc=1, device_id=device, device_id_type=MESH)
     pairs = [(context, cg.at[0, 0]), (out_weight_in, out_weight), (residual_in, residual), (gain_in, gain),
-             (router_in, router), (up_hbm, up), (down_hbm, down)]
+             (router_in, router)]
+    for k, at in enumerate([parity, 1 - parity]):
+        here, there = pl.ds(k * fold_cols, fold_cols), pl.ds(pl.multiple_of(at * fold_cols, fold_cols), fold_cols)
+        pairs += [(up_hbm.at[there], up.at[here]), (down_hbm.at[:, there], down.at[:, here])]
+    rest = pl.ds(2 * fold_cols, width - 2 * fold_cols)
+    pairs += [(up_hbm.at[rest], up.at[rest]), (down_hbm.at[:, rest], down.at[:, rest])]
     loads = [pltpu.make_async_copy(src, dst, wsem.at[i]) for i, (src, dst) in enumerate(pairs)]
     for load in loads:
         load.start()
@@ -252,14 +286,15 @@
     coming[1] = pass_on(0, 1, 1, down_z)
     loads[1].wait()
 
-    order = [0, 1, depth - 1, 2, depth - 2, 3, depth - 3, mid]
-    first = 5
+    wide = out_weight.shape[1] // 4
+    waves = [[0, 1, depth - 1], [2, depth - 2], [3, depth - 3, mid]]
+    order = [dz for wave in waves for dz in wave]
 
     def project(dz):
         for copy in shared[dz]:
             copy.wait_recv()
-        at_wave = order.index(dz)
-        p1, low = (wave_a[0], at_wave * 16) if at_wave < first else (wave_b[0], (at_wave - first) * 16)
+        k = [dz in wave for wave in waves].index(True)
+        p1, low = wave_bufs[k][0], waves[k].index(dz) * 16
         both = jnp.concatenate([cg[dz, 0], cg[dz, 1]], axis=0)
         res[...] = jnp.dot(both, out_weight[...], preferred_element_type=f32)
 
@@ -268,7 +303,9 @@
             home = lax.rem(x + dx, SIDE) * SIDE + lax.rem(y + dy, SIDE)
             at = pl.multiple_of(home * 8, 8)
             block = jnp.concatenate([res[pl.ds(at, 8), :], res[pl.ds(rows + at, 8), :]], axis=0)
-            p1[dx, dy, pl.ds(low, 16), :] = block.astype(bf16)
+            for quarter in range(4):
+                cols = slice(quarter * wide, (quarter + 1) * wide)
+                p1[quarter, dx, dy, pl.ds(low, 16), :] = block[:, cols].astype(bf16)
             return 0
 
         lax.fori_loop(0, SIDE * SIDE, body, 0)
@@ -289,7 +326,7 @@
             shared[b].append(hand_over(b, c))
         going, coming = going_next, coming_next
 
-    sum_a, sum_b = Sums(send, near, *wave_a), Sums(send, near, *wave_b)
+    early = [Sums(send, near, *buffers) for buffers in wave_bufs]
     both_halves = (0, 1)
 
     def each(step, *rest):
@@ -297,46 +334,51 @@
             for h in both_halves:
                 step(h, *args)
 
+    mine = r * depth + z
+    columns = {}
+
+    def to_tokens(k):
+        final = [early[k].s6(h) for h in both_halves]
+        for i, dz in enumerate(waves[k]):
+            for dr in (0, 1):
+                at = slice(i * 16 + dr * 8, i * 16 + dr * 8 + 8)
+                tiles[dz * 2 + dr] = jnp.concatenate([final[0][at], final[1][at]], axis=0).astype(bf16)
+        for dz in waves[k]:
+            for dr in (0, 1):
+                src, dst = tiles.at[dz * 2 + dr], heads.at[mine]
+                columns[dr, dz] = Local(src, dst) if (dr, dz) == (0, 0) else send(src, dst, peer(dr, dz))
+
+    w0, w1, w2 = early
     ring_step(1)
     project(0)
-    ring_step(2)
     project(depth - 1)
     project(1)
-    ring_step(3)
+    each(w0.s1, (0,), (1,))
+    ring_step(2)
     project(depth - 2)
     project(2)
-    each(sum_a.s1, (0,), (1,))
+    each(w1.s1, (0,), (1,))
+    each(w0.s2, (0,), (1,))
+    ring_step(3)
+    project(depth - 3)
+    project(3)
+    each(w0.s3)
     going[0].wait_recv()
     shared[mid] = [hand_over(mid, 0)]
     coming[1].wait_recv()
     shared[mid].append(hand_over(mid, 1))
-    project(depth - 3)
-    project(3)
-    each(sum_a.s2, (0,))
+    each(w1.s2, (0,), (1,))
     project(mid)
-    each(sum_b.s1, (0,), (1,))
-    each(sum_a.s2, (1,))
-    each(sum_a.s3)
-    each(sum_b.s2, (0,), (1,))
-    each(sum_a.s5)
-    each(sum_b.s3)
-    mine = r * depth + z
-    columns = {}
-
-    def to_tokens(total, dzs):
-        final = [total.s6(h) for h in both_halves]
-        for i, dz in enumerate(dzs):
-            for dr in (0, 1):
-                at = slice(i * 16 + dr * 8, i * 16 + dr * 8 + 8)
-                tiles[dz * 2 + dr] = jnp.concatenate([final[0][at], final[1][at]], axis=0).astype(bf16)
-        for dz in dzs:
-            for dr in (0, 1):
-                src, dst = tiles.at[dz * 2 + dr], heads.at[mine]
-                columns[dr, dz] = Local(src, dst) if (dr, dz) == (0, 0) else send(src, dst, peer(dr, dz))
-
-    to_tokens(sum_a, order[:first])
-    each(sum_b.s5)
-    to_tokens(sum_b, order[first:])
+    each(w2.s1, (0,), (1,))
+    each(w0.s5)
+    each(w1.s3)
+    each(w2.s2, (0,), (1,))
+    to_tokens(0)
+    each(w1.s5)
+    each(w2.s3)
+    to_tokens(1)
+    each(w2.s5)
+    to_tokens(2)
     for load in loads[2:5]:
         load.wait()
 
@@ -381,12 +423,14 @@
     for dr in (0, 1):
         for dz in range(depth):
             to = peer(dr, dz)
-            src, dst = outgoing.at[to[0] * EXPERTS + to[1] // halves], arrived.at[dr, dz]
+            src, dst = outgoing.at[to[0] * EXPERTS + to[1] // halves], arrived.at[dr, z]
             dispatched[dr, dz] = Local(src, dst) if (dr, dz) == (0, 0) else send(src, dst, to)
 
-    gathers = [Gather(send, near, grid.at[w]) for w in (0, 1)]
+    side_sent = [{}, {}]
+    gathers = [Gather(send, near, grid.at[w], fold_cols, twin) for w in (0, 1)]
     sums = [
-        Sums(send, near, part.at[w], rq.at[w], rf.at[w], rs.at[w], rq2.at[w], rf2.at[w]) for w in (0, 1)
+        Sums(send, near, part.at[w], rq.at[w], rf.at[w], rs.at[w], rq2.at[w], rf2.at[w], side_in.at[w], side_sent[w])
+        for w in (0, 1)
     ]
     slot_rows = 2 * depth
 
@@ -396,7 +440,9 @@
         block = arrived[w].reshape(8 * slot_rows, fold_cols)
         lines = jnp.dot(unfold[...], block, preferred_element_type=f32).astype(bf16)
         for j in range(8):
-            grid[w, 0, 0, :, pl.ds(j * fold_cols, fold_cols)] = lines[j * slot_rows : (j + 1) * slot_rows]
+            at = lax.rem(parity + j, 2) if j < 2 else j
+            cols = pl.ds(pl.multiple_of(at * fold_cols, fold_cols), fold_cols)
+            grid[w, 0, 0, :, cols] = lines[j * slot_rows : (j + 1) * slot_rows]
         gathers[w].begin()
 
     many = SIDE * SIDE * slot_rows
@@ -417,92 +463,101 @@
         if piece == 3:
             hidden[...] = jax.nn.gelu(acc[...]).astype(bf16)
 
+    def down_side(w):
+        side_chunk = fold_cols // 2
+
+        def body(i, _):
+            at = pl.ds(pl.multiple_of(i * side_chunk, side_chunk), side_chunk)
+            got = jnp.dot(hidden[...], down[:, at], preferred_element_type=f32)
+            got = got.astype(bf16).reshape(SIDE, SIDE, slot_rows, side_chunk)
+            for k in range(SIDE):
+                side_out[w, k, :, :, at] = got[:, k]
+            return 0
+
+        lax.fori_loop(0, 2, body, 0)
+        for k in (2, 3, 1, 0):
+            side_sent[w][k] = send(side_out.at[w, k], side_in.at[w, k], twin)
+
+    out_part = (width - fold_cols) // 4
+    out_chunk = out_part // 7
+
     def down_piece(w, quarter):
         def body(i, _):
-            at = pl.ds(pl.multiple_of(i * chunk, chunk), chunk)
+            here = pl.ds(pl.multiple_of(i * out_chunk, out_chunk), out_chunk)
+            at = pl.ds(pl.multiple_of(fold_cols + (quarter * 7 + i) * out_chunk, out_chunk), out_chunk)
             got = jnp.dot(hidden[...], down[:, at], preferred_element_type=f32)
-            part[w, :, :, :, at] = got.astype(bf16).reshape(SIDE, SIDE, slot_rows, chunk)
+            part[w, quarter, :, :, :, here] = got.astype(bf16).reshape(SIDE, SIDE, slot_rows, out_chunk)
             return 0
 
-        lax.fori_loop(quarter * 4, quarter * 4 + 4, body, 0)
+        lax.fori_loop(0, 7, body, 0)
 
     def down_and_send(w):
-        for quarter in (0, 1):
-            for h in (0, 1):
-                down_piece(w, 2 * h + quarter)
-                sums[w].s1(h, quarter)
+        down_side(w)
+        for h, quarter in ((1, 0), (0, 1), (1, 1), (0, 0)):
+            down_piece(w, 2 * h + quarter)
+            sums[w].s1(h, quarter)
 
     returns = {}
 
     def leave(w):
-        lines = []
-        for h in (0, 1):
-            total = sums[w].s6(h)
-            lines += [total[:, j * fold_cols : (j + 1) * fold_cols] for j in range(4)]
+        total = jnp.concatenate([sums[w].s6(h) for h in (0, 1)], axis=1)
+        mine_too = total[:, :fold_cols]
+        lines = [jnp.where(parity == k, 0.0, mine_too) for k in (0, 1)]
+        lines += [total[:, j * fold_cols : (j + 1) * fold_cols] for j in range(1, 7)]
         block = jnp.concatenate(lines, axis=0).astype(bf16)
         back[w] = (
             jnp.dot(fold[...], block, preferred_element_type=f32).astype(bf16).reshape(depth, slot_rows, fold_cols)
         )
         for dz in range(depth):
-            src, dst = back.at[w, dz], returned.at[mine]
+            src, dst = back.at[w, lax.rem(z - dz + depth, depth)], returned.at[mine]
             returns[w, dz] = Local(src, dst) if (w, dz) == (0, 0) else send(src, dst, peer(w, -dz))
 
     g0, g1 = gathers
     enter(0)
-    for h in (0, 1):
-        g0.step1(h)
-    for h in (0, 1):
-        g0.onward(h, 0)
-    for h in (0, 1):
-        g0.step3(h)
+    each(g0.step1)
+    each(g0.onward, (0,))
+    each(g0.step3)
     enter(1)
-    for a in (3, 1):
-        for h in (0, 1):
-            g0.onward(h, a)
-    for h in (0, 1):
-        g1.step1(h)
-    for h in (0, 1):
-        g0.onward(h, 2)
-    for h in (0, 1):
-        g1.onward(h, 0)
+    each(g0.onward, (3,), (1,))
+    g0.last(0)
+    each(g1.step1)
+    each(g0.onward, (2,))
+    g0.last(3)
+    g0.last(1)
+    each(g1.onward, (0,))
+    g0.last(2)
     g0.end()
-    loads[5].wait()
+    for i in (5, 7, 9):
+        loads[i].wait()
     up_piece(0, 0)
-    for h in (0, 1):
-        g1.step3(h)
+    each(g1.step3)
     up_piece(0, 1)
-    for h in (0, 1):
-        g1.onward(h, 3)
+    each(g1.onward, (3,))
     up_piece(0, 2)
-    for h in (0, 1):
-        g1.onward(h, 1)
+    each(g1.onward, (1,))
+    g1.last(0)
     up_piece(0, 3)
-    for h in (0, 1):
-        g1.onward(h, 2)
-    loads[6].wait()
+    each(g1.onward, (2,))
+    g1.last(3)
+    g1.last(1)
+    for i in (6, 8, 10):
+        loads[i].wait()
     down_and_send(0)
+    g1.last(2)
     g1.end()
     up_piece(1, 0)
-    for h in (0, 1):
-        sums[0].s2(h, 0)
+    each(sums[0].s2, (0,))
     up_piece(1, 1)
-    for h in (0, 1):
-        sums[0].s2(h, 1)
+    each(sums[0].s2, (1,))
     up_piece(1, 2)
     up_piece(1, 3)
-    for h in (0, 1):
-        sums[0].s3(h)
+    each(sums[0].s3)
     down_and_send(1)
-    for h in (0, 1):
-        sums[0].s5(h)
-    for quarter in (0, 1):
-        for h in (0, 1):
-            sums[1].s2(h, quarter)
+    each(sums[0].s5)
+    each(sums[1].s2, (0,), (1,))
     leave(0)
-    for h in (0, 1):
-        sums[1].s3(h)
-    for h in (0, 1):
-        sums[1].s5(h)
+    each(sums[1].s3)
+    each(sums[1].s5)
     leave(1)
     for w in (0, 1):
         for dz in range(depth):
@@ -527,18 +582,18 @@
     slot_rows = CAP * depth
     kinds = 2 * EXPERTS
     rows, group = context.shape[0], out_weight.shape[1]
-    q = width // 4
+    q = (width - fold_cols) // 4
     g4 = group // 4
     vm = pltpu.VMEM
 
     def sum_buffers(lines):
         return [
-            vm((4, 4, lines, group), bf16),
+            vm((4, 4, 4, lines, g4), bf16),
             vm((4, 4, lines, g4), bf16),
-            vm((2, 2, 4, lines, 2 * g4), bf16),
-            vm((2, 4, lines, 2 * g4), bf16),
+            vm((2, 2, 2, 4, lines, g4), bf16),
+            vm((2, 2, 4, lines, g4), bf16),
             vm((4, lines, g4), bf16),
-            vm((2, 2, lines, 2 * g4), bf16),
+            vm((2, 2, 2, lines, g4), bf16),
         ]
 
     scratch = [
@@ -552,8 +607,7 @@
         vm((8 * slot_rows, 8 * slot_rows), bf16),
         vm((depth, 2, rows, context.shape[1]), bf16),
         vm((2 * rows, group), f32),
-        sum_buffers(80),
-        sum_buffers(48),
+        [sum_buffers(48), sum_buffers(32), sum_buffers(48)],
         vm((2 * depth, 16, group // 2), bf16),
         vm((2 * depth, 16, group // 2), bf16),
         vm((tok_rows, width), f32),
@@ -565,17 +619,19 @@
         vm((hidden_units, width), bf16),
         vm((16 * slot_rows, hidden_units), f32),
         vm((16 * slot_rows, hidden_units), bf16),
-        vm((2, 4, 4, slot_rows, width), bf16),
+        vm((2, 4, 4, 4, slot_rows, q), bf16),
+        vm((2, 4, 4, slot_rows, fold_cols), bf16),
+        vm((2, 4, 4, slot_rows, fold_cols), bf16),
         vm((2, 4, 4, slot_rows, q), bf16),
-        vm((2, 2, 2, 4, slot_rows, 2 * q), bf16),
-        vm((2, 2, 4, slot_rows, 2 * q), bf16),
+        vm((2, 2, 2, 2, 4, slot_rows, q), bf16),
+        vm((2, 2, 2, 4, slot_rows, q), bf16),
         vm((2, 4, slot_rows, q), bf16),
-        vm((2, 2, 2, slot_rows, 2 * q), bf16),
+        vm((2, 2, 2, 2, slot_rows, q), bf16),
         vm((2, depth, CAP * 8, fold_cols), bf16),
         vm((2 * depth, CAP * 8, fold_cols), bf16),
         pltpu.SemaphoreType.DMA((NSEM,)),
         pltpu.SemaphoreType.DMA((NSEM,)),
-        pltpu.SemaphoreType.DMA((7,)),
+        pltpu.SemaphoreType.DMA((11,)),
     ]
     local = pl.BlockSpec(memory_space=pltpu.VMEM)
     there = pl.BlockSpec(memory_space=pl.ANY)

time: 171 us -> 170 us (level)
  no operation moved by 1% of the time
where the time goes in v3:
time: 170 us
  Pallas kernels  169 us (99%)
    pallas_call x1, Pallas kernels, per_device(): pl.pallas_call(functools.partial(kernel, depth), out_shape=jax.ShapeDtype...  169 us

profile of v3, /device:TPU:1, one launch (start us, length us, event | category | flops | bytes accessed | tf_op | source)
XLA Modules:
  0.0 170.1 jit_solution(17962290985218640472)
XLA Ops:
  0.0 168.5 %shard_map.91 = bf16[8,8192]{1,0:T(8,128)(2,1)} custom-call(s32[8]{0:T(128)} %modality.1, s32[8]{0:T(128)} %expert.1, bf16[8,8192]{1,0:T(8,128)(2,1)} %residual_in.1, bf16[128,512]{1,0:T(8,128)(2,1)} %context.1, bf16[512,512]{1,0:T(8,128)(2,1)} %out_weight_in.1, bf16[64,128]{1,0:T(8,128)(2,1)} %bitcast.5, bf16[2,4,8192]{2,1,0:T(4,128)(2,1)} %router_in.1, ...), custom_call_target="tpu_custom_call" | custom-call | tf_op jit(solution)/shard_map/pallas_call | solution.py:638
  168.5 1.6 copy.11

commit v4 on v3

--- a/solution.py
+++ b/solution.py
@@ -11,7 +11,7 @@
 CAP = 2
 EPSILON = 1e-05
 SIDE = 4
-NSEM = 320
+NSEM = 496
 f32, bf16 = jnp.float32, jnp.bfloat16
 MESH = pl.DeviceIdType.MESH
 
@@ -181,8 +181,8 @@
 
 def kernel(
     depth, modality, expert, residual_in, context, out_weight_in, gain_in, router_in, up_hbm, down_hbm, out,
-    residual, out_weight, gain, router, pick, put, unfold, fold, cg, res, wave_bufs, tiles, heads, resid, folded,
-    outgoing, arrived, grid, up, down, acc, hidden, part, side_out, side_in, rq, rf, rs, rq2, rf2, back, returned, ssem, rsem, wsem,
+    residual, out_weight, gain, router, put, fold, fold_small, tags, tags_in, residual_cols, cg, res, wave_bufs, stack, tiles, heads,
+    resid, outgoing, arrived, grid, up, down, acc, hidden, part, back, returned, ssem, rsem, wsem,
 ):
     r, z, t = lax.axis_index("role"), lax.axis_index("exp"), lax.axis_index("tp")
     x, y = t // SIDE, t % SIDE
@@ -191,11 +191,16 @@
     count = [0]
     sent = []
 
-    def send(src, dst, device):
+    def send(src, dst, device, landed=None):
         k = count[0]
         count[0] += 1
         copy = pltpu.make_async_remote_copy(
-            src_ref=src, dst_ref=dst, send_sem=ssem.at[k], recv_sem=rsem.at[k], device_id=device, device_id_type=MESH
+            src_ref=src,
+            dst_ref=dst,
+            send_sem=ssem.at[k],
+            recv_sem=rsem.at[k] if landed is None else landed,
+            device_id=device,
+            device_id_type=MESH,
         )
         copy.start()
         sent.append(copy)
@@ -255,16 +260,16 @@
     def table(shape):
         return (lax.broadcasted_iota(jnp.int32, shape, 0), lax.broadcasted_iota(jnp.int32, shape, 1))
 
-    row, col = table(pick.shape)
-    pick[...] = jnp.where(((row >> 3) == spread(slot_of, col & 7)) & ((row & 7) == (col >> 3)), 1.0, 0.0).astype(bf16)
     row, col = table(put.shape)
     slot = (col >> 5) * 2 + ((col >> 3) & 1)
     put[...] = jnp.where((slot == spread(slot_of, row & 7)) & ((col & 7) == (row >> 3)), 1.0, 0.0).astype(bf16)
-    row, col = table(unfold.shape)
-    unfold[...] = jnp.where(((row & 15) >> 1) * 16 + (row & 1) * 8 + (row >> 4) == col, 1.0, 0.0).astype(bf16)
+    row, col = table(fold.shape)
     fold[...] = jnp.where(((col & 15) >> 1) * 16 + (col & 1) * 8 + (col >> 4) == row, 1.0, 0.0).astype(bf16)
+    row, col = table(fold_small.shape)
+    fold_small[...] = jnp.where(((col & 7) >> 1) * 16 + (col & 1) * 8 + (col >> 3) == row, 1.0, 0.0).astype(bf16)
     row, col = table((8, 1))
     route_rows = spread(routes, row)
+    tags[...] = spread(slot_of, table(tags.shape)[1] & 7).astype(f32)
     loads[0].wait()
     pl.semaphore_wait(barrier, len(others))
 
@@ -335,15 +340,28 @@
                 step(h, *args)
 
     mine = r * depth + z
-    columns = {}
+    columns, extras = {}, {}
+    group = width // (2 * depth)
 
     def to_tokens(k):
         final = [early[k].s6(h) for h in both_halves]
         for i, dz in enumerate(waves[k]):
+            pair = []
             for dr in (0, 1):
                 at = slice(i * 16 + dr * 8, i * 16 + dr * 8 + 8)
-                tiles[dz * 2 + dr] = jnp.concatenate([final[0][at], final[1][at]], axis=0).astype(bf16)
-        for dz in waves[k]:
+                if dz == 0 and dr == 0:
+                    cols = pl.ds(pl.multiple_of(mine * group, group), group)
+                    own = residual[:, cols].astype(f32)
+                else:
+                    extras[dr, -dz % depth][1].wait_recv()
+                    own = residual_cols[dr, -dz % depth].astype(f32)
+                value = (own + jnp.concatenate([final[0][at], final[1][at]], axis=1)).astype(bf16)
+                tiles[dz * 2 + dr] = value
+                pair.append(value.astype(f32))
+            stack[pl.ds(dz * 16, 16), :] = jnp.concatenate(pair, axis=0).astype(bf16)
+
+    def resid_to_tokens():
+        for dz in range(depth):
             for dr in (0, 1):
                 src, dst = tiles.at[dz * 2 + dr], heads.at[mine]
                 columns[dr, dz] = Local(src, dst) if (dr, dz) == (0, 0) else send(src, dst, peer(dr, dz))
@@ -368,6 +386,16 @@
     coming[1].wait_recv()
     shared[mid].append(hand_over(mid, 1))
     each(w1.s2, (0,), (1,))
+    loads[2].wait()
+    for dz in range(depth):
+        for dr in (0, 1):
+            if (dr, dz) != (0, 0):
+                to = peer(dr, dz)
+                cols = pl.ds(pl.multiple_of((to[0] * depth + to[1]) * group, group), group)
+                extras[dr, dz] = (
+                    send(tags, tags_in.at[dr, dz], to),
+                    send(residual.at[:, cols], residual_cols.at[dr, dz], to),
+                )
     project(mid)
     each(w2.s1, (0,), (1,))
     each(w0.s5)
@@ -379,125 +407,155 @@
     to_tokens(1)
     each(w2.s5)
     to_tokens(2)
-    for load in loads[2:5]:
+
+    shares = [(0, 16), (16, 8), (24, 8)]
+    all_waves = range(len(shares))
+    lane = lax.broadcasted_iota(jnp.int32, (1, 16 * depth), 1)
+    tag = jnp.zeros((1, 16 * depth), f32)
+    for dz in range(depth):
+        for dr in (0, 1):
+            if (dr, dz) == (0, 0):
+                got = tags[...]
+            else:
+                extras[dr, dz][0].wait_recv()
+                got = tags_in[dr, dz]
+            tag = jnp.where((lane >> 3) == (-dz % depth) * 2 + dr, got[0:1], tag)
+    row, col = table((2 * EXPERTS * 2 * CAP * depth, 16 * depth))
+    kind, wave, from_z, place = row >> 5, (row >> 4) & 1, (row & 15) >> 1, row & 1
+    token_z = (z + (col >> 4)) & (depth - 1)
+    token_wave = (r + ((col >> 3) & 1) + kind // EXPERTS) & 1
+    fits = (tag == (kind * CAP + place).astype(f32)) & (token_z == from_z) & (token_wave == wave)
+    slots = jnp.dot(jnp.where(fits, 1.0, 0.0).astype(bf16), stack[...], preferred_element_type=f32)
+    by_kind = slots.reshape(2 * EXPERTS, 4 * depth, group)
+    for w, (low, size) in enumerate(shares):
+        outgoing[w][...] = by_kind[:, low : low + size].astype(bf16)
+    halves = depth // EXPERTS
+    dispatched = {}
+    for w in all_waves:
+        for dz in range(depth):
+            for dr in (0, 1):
+                to = peer(dr, dz)
+                src = outgoing[w].at[to[0] * EXPERTS + to[1] // halves]
+                dst = arrived[w].at[mine]
+                dispatched[w, dr, dz] = Local(src, dst) if (dr, dz) == (0, 0) else send(src, dst, to)
+    resid_to_tokens()
+    for load in loads[3:5]:
         load.wait()
 
-    group = width // (2 * depth)
-    squares = jnp.zeros((8, group), f32)
-    for dz in order:
-        for dr in (0, 1):
-            columns[dr, dz].wait_recv()
-            source = lax.rem(r + dr, 2) * depth + lax.rem(z - dz + depth, depth)
-            block = heads[source].astype(f32)
-            whole = jnp.concatenate([block[:8], block[8:]], axis=1)
-            cols = pl.ds(pl.multiple_of(source * group, group), group)
-            value = (residual[:, cols].astype(f32) + whole).astype(bf16).astype(f32)
-            resid[:, cols] = value
+    def tokens():
+        squares = jnp.zeros((8, group), f32)
+        for dz in range(depth):
+            for dr in (0, 1):
+                columns[dr, dz].wait_recv()
+        for g in range(2 * depth):
+            value = heads[g].astype(f32)
+            resid[:, g * group : (g + 1) * group] = value
             squares = squares + value * value
-    inverse = lax.rsqrt(jnp.sum(squares, axis=1, keepdims=True) / width + EPSILON)
-    logits = jnp.zeros((8, fold_cols), f32)
-    lanes = gain.shape[1]
-    per_fold = fold_cols // lanes
-    for j in range(0, 8, 2):
-        pair = []
-        for i in (j, j + 1):
-            cols = slice(i * fold_cols, (i + 1) * fold_cols)
-            gains = gain[pl.ds(i * per_fold, per_fold), :].astype(f32)
-            gains = jnp.concatenate(
-                [jnp.broadcast_to(gains[k : k + 1], (8, lanes)) for k in range(per_fold)], axis=1
-            )
-            normed = (resid[:, cols] * inverse * gains).astype(bf16).astype(f32)
-            picked = jnp.zeros((8, fold_cols), f32)
+        inverse = lax.rsqrt(jnp.sum(squares, axis=1, keepdims=True) / width + EPSILON)
+        logits = jnp.zeros((8, group), f32)
+        for g in range(2 * depth):
+            cols = slice(g * group, (g + 1) * group)
+            normed = (resid[:, cols] * inverse * gains_of(g, 8)).astype(bf16).astype(f32)
+            picked = jnp.zeros((8, group), f32)
             for e in range(2 * EXPERTS):
                 line = router[e // EXPERTS, :, cols].astype(f32)[e % EXPERTS : e % EXPERTS + 1]
                 picked = jnp.where(route_rows == e, line, picked)
             logits = logits + normed * picked
-            pair.append(normed)
-        folded[pl.ds(j * 8, 16), :] = jnp.concatenate(pair, axis=0).astype(bf16)
-    slots = jnp.dot(pick[...], folded[...], preferred_element_type=f32).astype(bf16)
-    outgoing[...] = slots.reshape(outgoing.shape)
-    gating = jax.nn.sigmoid(jnp.sum(logits, axis=1, keepdims=True))
-
-    halves = depth // EXPERTS
-    dispatched = {}
-    for dr in (0, 1):
+        return jax.nn.sigmoid(jnp.sum(logits, axis=1, keepdims=True))
+
+    lanes = gain.shape[1]
+    per_group = group // lanes
+
+    def gains_of(g, lines):
+        rows_of = gain[pl.ds(g // 2 * 2 * per_group, 2 * per_group), :].astype(f32)
+        first = g % 2 * per_group
+        return jnp.concatenate(
+            [jnp.broadcast_to(rows_of[first + k : first + k + 1], (lines, lanes)) for k in range(per_group)], axis=1
+        )
+
+    side_sent = [{} for _ in all_waves]
+    gathers = [Gather(send, near, grid[w], fold_cols, twin) for w in all_waves]
+    sums = [Sums(send, near, *part[w][:6], part[w][7], side_sent[w]) for w in all_waves]
+
+    def enter(w):
+        lines = shares[w][1]
+        squares = jnp.zeros((lines, group), f32)
         for dz in range(depth):
-            to = peer(dr, dz)
-            src, dst = outgoing.at[to[0] * EXPERTS + to[1] // halves], arrived.at[dr, z]
-            dispatched[dr, dz] = Local(src, dst) if (dr, dz) == (0, 0) else send(src, dst, to)
-
-    side_sent = [{}, {}]
-    gathers = [Gather(send, near, grid.at[w], fold_cols, twin) for w in (0, 1)]
-    sums = [
-        Sums(send, near, part.at[w], rq.at[w], rf.at[w], rs.at[w], rq2.at[w], rf2.at[w], side_in.at[w], side_sent[w])
-        for w in (0, 1)
-    ]
-    slot_rows = 2 * depth
-
-    def enter(w):
-        for dz in range(depth):
-            dispatched[w, dz].wait_recv()
-        block = arrived[w].reshape(8 * slot_rows, fold_cols)
-        lines = jnp.dot(unfold[...], block, preferred_element_type=f32).astype(bf16)
-        for j in range(8):
-            at = lax.rem(parity + j, 2) if j < 2 else j
-            cols = pl.ds(pl.multiple_of(at * fold_cols, fold_cols), fold_cols)
-            grid[w, 0, 0, :, cols] = lines[j * slot_rows : (j + 1) * slot_rows]
+            for dr in (0, 1):
+                dispatched[w, dr, dz].wait_recv()
+        for g in range(2 * depth):
+            value = arrived[w][g].astype(f32)
+            squares = squares + value * value
+        inverse = lax.rsqrt(jnp.sum(squares, axis=1, keepdims=True) / width + EPSILON)
+        for g in range(2 * depth):
+            normed = (arrived[w][g].astype(f32) * inverse * gains_of(g, lines)).astype(bf16)
+            at = g * group
+            if g < 4:
+                at = lax.rem(parity + g // 2, 2) * fold_cols + g % 2 * group
+                at = pl.multiple_of(at, group)
+            grid[w][0, 0, :, pl.ds(at, group)] = normed
         gathers[w].begin()
 
-    many = SIDE * SIDE * slot_rows
     chunk = width // 16
 
-    def up_piece(w, piece):
-        if piece == 0:
-            acc[...] = jnp.zeros_like(acc)
+    def up_piece(w, low, high):
+        many = SIDE * SIDE * shares[w][1]
+        total = acc.at[pl.ds(0, many)]
+        if low == 0:
+            total[...] = jnp.zeros((many, acc.shape[1]), f32)
 
         def body(i, _):
             at = pl.ds(pl.multiple_of(i * chunk, chunk), chunk)
-            acc[...] += jnp.dot(
-                grid[w, :, :, :, at].reshape(many, chunk), up[at, :], preferred_element_type=f32
-            )
+            lines = grid[w][:, :, :, at]
+            if shares[w][1] % 16:
+                lines = lines.astype(f32).reshape(many, chunk).astype(bf16)
+            else:
+                lines = lines.reshape(many, chunk)
+            total[...] += jnp.dot(lines, up[at, :], preferred_element_type=f32)
             return 0
 
-        lax.fori_loop(piece * 4, piece * 4 + 4, body, 0)
-        if piece == 3:
-            hidden[...] = jax.nn.gelu(acc[...]).astype(bf16)
+        lax.fori_loop(low, high, body, 0)
+        if high == 16:
+            hidden[pl.ds(0, many), :] = jax.nn.gelu(total[...]).astype(bf16)
+
+    def product(w, at):
+        lines = shares[w][1]
+        got = jnp.dot(hidden[pl.ds(0, 16 * lines), :], down[:, at], preferred_element_type=f32)
+        return got.reshape(SIDE, SIDE, lines, got.shape[1]).astype(bf16)
 
     def down_side(w):
         side_chunk = fold_cols // 2
+        side_out, side_in = part[w][6:]
 
         def body(i, _):
             at = pl.ds(pl.multiple_of(i * side_chunk, side_chunk), side_chunk)
-            got = jnp.dot(hidden[...], down[:, at], preferred_element_type=f32)
-            got = got.astype(bf16).reshape(SIDE, SIDE, slot_rows, side_chunk)
+            got = product(w, at)
             for k in range(SIDE):
-                side_out[w, k, :, :, at] = got[:, k]
+                side_out[k, :, :, at] = got[:, k]
             return 0
 
         lax.fori_loop(0, 2, body, 0)
         for k in (2, 3, 1, 0):
-            side_sent[w][k] = send(side_out.at[w, k], side_in.at[w, k], twin)
-
-    out_part = (width - fold_cols) // 4
-    out_chunk = out_part // 7
+            side_sent[w][k] = send(side_out.at[k], side_in.at[k], twin)
+
+    out_chunk = (width - fold_cols) // 4 // 7
 
     def down_piece(w, quarter):
         def body(i, _):
             here = pl.ds(pl.multiple_of(i * out_chunk, out_chunk), out_chunk)
             at = pl.ds(pl.multiple_of(fold_cols + (quarter * 7 + i) * out_chunk, out_chunk), out_chunk)
-            got = jnp.dot(hidden[...], down[:, at], preferred_element_type=f32)
-            part[w, quarter, :, :, :, here] = got.astype(bf16).reshape(SIDE, SIDE, slot_rows, out_chunk)
+            part[w][0][quarter, :, :, :, here] = product(w, at)
             return 0
 
         lax.fori_loop(0, 7, body, 0)
 
-    def down_and_send(w):
-        down_side(w)
-        for h, quarter in ((1, 0), (0, 1), (1, 1), (0, 0)):
-            down_piece(w, 2 * h + quarter)
-            sums[w].s1(h, quarter)
+    def down_and_send(w, h, quarter):
+        down_piece(w, 2 * h + quarter)
+        sums[w].s1(h, quarter)
 
     returns = {}
+    landed = [rsem.at[NSEM - depth + k] for k in range(depth)]
+    my_landed = rsem.at[NSEM - depth + z]
 
     def leave(w):
         total = jnp.concatenate([sums[w].s6(h) for h in (0, 1)], axis=1)
@@ -505,14 +563,21 @@
         lines = [jnp.where(parity == k, 0.0, mine_too) for k in (0, 1)]
         lines += [total[:, j * fold_cols : (j + 1) * fold_cols] for j in range(1, 7)]
         block = jnp.concatenate(lines, axis=0).astype(bf16)
-        back[w] = (
-            jnp.dot(fold[...], block, preferred_element_type=f32).astype(bf16).reshape(depth, slot_rows, fold_cols)
-        )
-        for dz in range(depth):
-            src, dst = back.at[w, lax.rem(z - dz + depth, depth)], returned.at[mine]
-            returns[w, dz] = Local(src, dst) if (w, dz) == (0, 0) else send(src, dst, peer(w, -dz))
-
-    g0, g1 = gathers
+        by = fold if w == 0 else fold_small
+        sorted_lines = jnp.dot(by[...], block, preferred_element_type=f32).astype(bf16)
+        back[w][...] = sorted_lines.reshape(back[w].shape)
+        dst = returned.at[mine]
+        if w == 0:
+            for dz in range(depth):
+                src = back[0].at[lax.rem(z - dz + depth, depth)]
+                returns[dz] = Local(src, dst) if dz == 0 else send(src, dst, peer(0, -dz))
+        else:
+            for k in range(depth // 2):
+                to = (lax.rem(r + 1, 2), (w - 1) * (depth // 2) + k, t)
+                returns[w, k] = send(back[w].at[k], dst, to, my_landed)
+
+    g0, g1, g2 = gathers
+    v0, v1, v2 = sums
     enter(0)
     each(g0.step1)
     each(g0.onward, (0,))
@@ -520,56 +585,103 @@
     enter(1)
     each(g0.onward, (3,), (1,))
     g0.last(0)
+    enter(2)
     each(g1.step1)
     each(g0.onward, (2,))
     g0.last(3)
     g0.last(1)
     each(g1.onward, (0,))
+    each(g2.step1)
     g0.last(2)
     g0.end()
     for i in (5, 7, 9):
         loads[i].wait()
-    up_piece(0, 0)
+    up_piece(0, 0, 4)
     each(g1.step3)
-    up_piece(0, 1)
-    each(g1.onward, (3,))
-    up_piece(0, 2)
-    each(g1.onward, (1,))
+    each(g2.onward, (0,))
+    up_piece(0, 4, 8)
+    each(g1.onward, (3,), (1,))
+    each(g2.step3)
     g1.last(0)
-    up_piece(0, 3)
+    up_piece(0, 8, 12)
     each(g1.onward, (2,))
     g1.last(3)
     g1.last(1)
+    each(g2.onward, (3,))
+    up_piece(0, 12, 16)
+    each(g2.onward, (1,))
+    g2.last(0)
+    g1.last(2)
     for i in (6, 8, 10):
         loads[i].wait()
-    down_and_send(0)
-    g1.last(2)
+    down_side(0)
+    down_and_send(0, 1, 0)
+    each(g2.onward, (2,))
+    g2.last(3)
+    g2.last(1)
+    down_and_send(0, 0, 1)
     g1.end()
-    up_piece(1, 0)
-    each(sums[0].s2, (0,))
-    up_piece(1, 1)
-    each(sums[0].s2, (1,))
-    up_piece(1, 2)
-    up_piece(1, 3)
-    each(sums[0].s3)
-    down_and_send(1)
-    each(sums[0].s5)
-    each(sums[1].s2, (0,), (1,))
+    down_and_send(0, 1, 1)
+    g2.last(2)
+    down_piece(0, 0)
+    up_piece(1, 0, 8)
+    v0.s2(1, 0)
+    v0.s1(0, 0)
+    up_piece(1, 8, 16)
+    v0.s2(0, 1)
+    v0.s2(1, 1)
+    g2.end()
+    down_side(1)
+    down_and_send(1, 1, 0)
+    down_and_send(1, 0, 1)
+    v0.s2(0, 0)
+    down_and_send(1, 1, 1)
+    down_piece(1, 0)
+    v0.s3(1)
+    up_piece(2, 0, 8)
+    v1.s1(0, 0)
+    v1.s2(1, 0)
+    up_piece(2, 8, 16)
+    v0.s3(0)
+    down_side(2)
+    down_and_send(2, 1, 0)
+    v1.s2(0, 1)
+    down_and_send(2, 0, 1)
+    v1.s2(1, 1)
+    down_and_send(2, 1, 1)
+    down_piece(2, 0)
+    v0.s5(1)
+    v1.s2(0, 0)
+    v0.s5(0)
+    gating = tokens()
+    v1.s3(1)
+    v2.s1(0, 0)
+    v2.s2(1, 0)
     leave(0)
-    each(sums[1].s3)
-    each(sums[1].s5)
+    v1.s3(0)
+    v2.s2(0, 1)
+    v1.s5(1)
+    v2.s2(1, 1)
+    v1.s5(0)
+    v2.s2(0, 0)
+    v2.s3(1)
     leave(1)
-    for w in (0, 1):
-        for dz in range(depth):
-            returns[w, dz].wait_recv()
-    block = returned[...].reshape(2 * depth * slot_rows, fold_cols)
+    v2.s5(1)
+    v2.s3(0)
+    v2.s5(0)
+    leave(2)
+    for dz in range(depth):
+        returns[dz].wait_recv()
+    for k in range(depth):
+        pltpu.make_async_copy(back[1].at[0], returned.at[0], landed[k]).wait()
+    block = returned[...].reshape(2 * depth * 8 * CAP, fold_cols)
     experts = jnp.dot(put[...], block, preferred_element_type=f32)
     for j in range(8):
         cols = slice(j * fold_cols, (j + 1) * fold_cols)
         out[:, cols] = (resid[:, cols] + gating * experts[j * 8 : j * 8 + 8]).astype(bf16)
     for copy in sent:
         copy.wait_send()
-    assert count[0] <= NSEM
+    assert count[0] <= NSEM - depth
 
 
 def per_device(
@@ -586,14 +698,14 @@
     g4 = group // 4
     vm = pltpu.VMEM
 
-    def sum_buffers(lines):
+    def sum_buffers(lines, cols):
         return [
-            vm((4, 4, 4, lines, g4), bf16),
-            vm((4, 4, lines, g4), bf16),
-            vm((2, 2, 2, 4, lines, g4), bf16),
-            vm((2, 2, 4, lines, g4), bf16),
-            vm((4, lines, g4), bf16),
-            vm((2, 2, 2, lines, g4), bf16),
+            vm((4, 4, 4, lines, cols), bf16),
+            vm((4, 4, lines, cols), bf16),
+            vm((2, 2, 2, 4, lines, cols), bf16),
+            vm((2, 2, 4, lines, cols), bf16),
+            vm((4, lines, cols), bf16),
+            vm((2, 2, 2, lines, cols), bf16),
         ]
 
     scratch = [
@@ -601,33 +713,31 @@
         vm(out_weight.shape, bf16),
         vm((width // 128, 128), bf16),
         vm(router.shape, bf16),
-        vm((kinds * CAP * 8, 8 * tok_rows), bf16),
         vm((8 * tok_rows, 2 * depth * CAP * 8), bf16),
         vm((8 * slot_rows, 8 * slot_rows), bf16),
-        vm((8 * slot_rows, 8 * slot_rows), bf16),
+        vm((4 * slot_rows, 4 * slot_rows), bf16),
+        vm((8, 128), f32),
+        vm((2, depth, 8, 128), f32),
+        vm((2, depth, tok_rows, group), bf16),
         vm((depth, 2, rows, context.shape[1]), bf16),
         vm((2 * rows, group), f32),
-        [sum_buffers(48), sum_buffers(32), sum_buffers(48)],
-        vm((2 * depth, 16, group // 2), bf16),
-        vm((2 * depth, 16, group // 2), bf16),
+        [sum_buffers(48, g4), sum_buffers(32, g4), sum_buffers(48, g4)],
+        vm((16 * depth, group), bf16),
+        vm((2 * depth, tok_rows, group), bf16),
+        vm((2 * depth, tok_rows, group), bf16),
         vm((tok_rows, width), f32),
-        vm((8 * tok_rows, fold_cols), bf16),
-        vm((kinds, CAP * 8, fold_cols), bf16),
-        vm((2, depth, CAP * 8, fold_cols), bf16),
-        vm((2, 4, 4, slot_rows, width), bf16),
+        [vm((kinds, n, group), bf16) for n in (16, 8, 8)],
+        [vm((2 * depth, n, group), bf16) for n in (16, 8, 8)],
+        [vm((4, 4, n, width), bf16) for n in (16, 8, 8)],
         vm((width, hidden_units), bf16),
         vm((hidden_units, width), bf16),
         vm((16 * slot_rows, hidden_units), f32),
         vm((16 * slot_rows, hidden_units), bf16),
-        vm((2, 4, 4, 4, slot_rows, q), bf16),
-        vm((2, 4, 4, slot_rows, fold_cols), bf16),
-        vm((2, 4, 4, slot_rows, fold_cols), bf16),
-        vm((2, 4, 4, slot_rows, q), bf16),
-        vm((2, 2, 2, 2, 4, slot_rows, q), bf16),
-        vm((2, 2, 2, 4, slot_rows, q), bf16),
-        vm((2, 4, slot_rows, q), bf16),
-        vm((2, 2, 2, 2, slot_rows, q), bf16),
-        vm((2, depth, CAP * 8, fold_cols), bf16),
+        [
+            sum_buffers(n, q) + [vm((4, 4, n, fold_cols), bf16), vm((4, 4, n, fold_cols), bf16)]
+            for n in (16, 8, 8)
+        ],
+        [vm((n, CAP * 8, fold_cols), bf16) for n in (8, 4, 4)],
         vm((2 * depth, CAP * 8, fold_cols), bf16),
         pltpu.SemaphoreType.DMA((NSEM,)),
         pltpu.SemaphoreType.DMA((NSEM,)),

time: 170 us -> 165 us (0.971)
  the two profiles are of different devices: /device:TPU:1 before, /device:TPU:193 now
where the time goes in v4:
time: 165 us
  Pallas kernels  163 us (99%)
    pallas_call x1, Pallas kernels, per_device(): pl.pallas_call(functools.partial(kernel, depth), out_shape=jax.ShapeDtype...  163 us

profile of v4, /device:TPU:193, one launch (start us, length us, event | category | flops | bytes accessed | tf_op | source)
XLA Modules:
  0.0 165.0 jit_solution(303065201544670653)
XLA Ops:
  0.0 163.4 %shard_map.91 = bf16[8,8192]{1,0:T(8,128)(2,1)} custom-call(s32[8]{0:T(128)} %modality.1, s32[8]{0:T(128)} %expert.1, bf16[8,8192]{1,0:T(8,128)(2,1)} %residual_in.1, bf16[128,512]{1,0:T(8,128)(2,1)} %context.1, bf16[512,512]{1,0:T(8,128)(2,1)} %out_weight_in.1, bf16[64,128]{1,0:T(8,128)(2,1)} %bitcast.5, bf16[2,4,8192]{2,1,0:T(4,128)(2,1)} %router_in.1, ...), custom_call_target="tpu_custom_call" | custom-call | tf_op jit(solution)/shard_map/pallas_call | solution.py:748
  163.4 1.6 copy.11

commit v5 on v4

--- a/solution.py
+++ b/solution.py
@@ -228,7 +228,7 @@
     parity = lax.rem(z, 2)
     twin = (r, z + 1 - 2 * parity, t)
     barrier = pltpu.get_barrier_semaphore()
-    others = [peer(dr, dz) for dz in range(depth) for dr in (0, 1) if (dr, dz) != (0, 0)]
+    others = [peer(1, 0), peer(0, 1), peer(0, -1)]
     others += [near(axis, step) for axis in (0, 1) for step in (1, -1)]
     for device in others:
         pl.semaphore_signal(barrier, inc=1, device_id=device, device_id_type=MESH)
@@ -386,6 +386,7 @@
     coming[1].wait_recv()
     shared[mid].append(hand_over(mid, 1))
     each(w1.s2, (0,), (1,))
+    project(mid)
     loads[2].wait()
     for dz in range(depth):
         for dr in (0, 1):
@@ -396,7 +397,6 @@
                     send(tags, tags_in.at[dr, dz], to),
                     send(residual.at[:, cols], residual_cols.at[dr, dz], to),
                 )
-    project(mid)
     each(w2.s1, (0,), (1,))
     each(w0.s5)
     each(w1.s3)
@@ -653,7 +653,6 @@
     v0.s5(1)
     v1.s2(0, 0)
     v0.s5(0)
-    gating = tokens()
     v1.s3(1)
     v2.s1(0, 0)
     v2.s2(1, 0)
@@ -668,6 +667,7 @@
     leave(1)
     v2.s5(1)
     v2.s3(0)
+    gating = tokens()
     v2.s5(0)
     leave(2)
     for dz in range(depth):

time: 165 us -> 163 us (0.988)
  the two profiles are of different devices: /device:TPU:193 before, /device:TPU:201 now
where the time goes in v5:
time: 163 us
  Pallas kernels  162 us (99%)
    pallas_call x1, Pallas kernels, per_device(): pl.pallas_call(functools.partial(kernel, depth), out_shape=jax.ShapeDtype...  162 us

profile of v5, /device:TPU:201, one launch (start us, length us, event | category | flops | bytes accessed | tf_op | source)
XLA Modules:
  0.0 163.4 jit_solution(2068670626782405303)
XLA Ops:
  0.0 161.8 %shard_map.91 = bf16[8,8192]{1,0:T(8,128)(2,1)} custom-call(s32[8]{0:T(128)} %modality.1, s32[8]{0:T(128)} %expert.1, bf16[8,8192]{1,0:T(8,128)(2,1)} %residual_in.1, bf16[128,512]{1,0:T(8,128)(2,1)} %context.1, bf16[512,512]{1,0:T(8,128)(2,1)} %out_weight_in.1, bf16[64,128]{1,0:T(8,128)(2,1)} %bitcast.5, bf16[2,4,8192]{2,1,0:T(4,128)(2,1)} %router_in.1, ...), custom_call_target="tpu_custom_call" | custom-call | tf_op jit(solution)/shard_map/pallas_call | solution.py:748
  161.8 1.6 copy.11
